TPU v7x, 32 devices: a whole 2x2x4 slice. The times are simulated.
32 devices in a mesh: row: 8 (over z, core), col: 4 (over y, x).
Axes of the slice: x: 2, y: 2, z: 4, core: 2. Of those that a mesh axis runs over, the one named last changes fastest.
Arguments:
- source: float32 [16, 256, 512], P(None, 'row', 'col'), may hold values from -6 to 6
- guess: float32 [16, 256, 512], P(None, 'row', 'col'), may hold values from -6 to 6
- conductivity: float32 [256, 512], P('row', 'col'), may hold values from 0.1 to 10
- storage: float32 [256, 512], P('row', 'col'), may hold values from 0.02 to 0.2
- aggregates: int32 [256, 512], P('row', 'col'), may hold values from 0 to 63, as said below
- pair_maps: int32 [4, 8, 4, 128], P(None, 'row', 'col'), may hold values from 0 to 63, as said below
Outputs:
- solution: float32 [16, 256, 512], P(None, 'row', 'col')
- residual: float32 [16, 256, 512], P(None, 'row', 'col')
Inputs may be any that keep to these rules, and one draw needn't show every extreme that they name: `aggregates`: within each tile of 32 x 128 cells every id from 0 to 63 names exactly 64 cells of that tile. pair_maps[k, r, c] is the same for all tiles of one group of agglomeration level k + 1, that is all tiles whose row index shifted right by (k + 1) // 2 bits and column index shifted right by (k + 2) // 2 bits agree; each coarse unknown receives exactly two of the 128 entries.
All inputs are finite; a program needn't handle non-finite values.
Results may differ from a plain program's by a relative error of at most 0.0003.
Values sent between devices are 32-bit elements; how exact they have to be, the bound alone decides.
A program may use at most 64 MiB of HBM per device.

v0:
```python
from functools import partial

import jax
import jax.numpy as jnp
from jax import lax
from jax.sharding import PartitionSpec as P

NA = 64
SWEEPS = 3
LEVELS = 4


OMEGA_FINE = 0.8
OMEGA_COARSE = 0.6
HIGHEST = lax.Precision.HIGHEST


def with_halo(cells, sides, width):
    for axis, dim in sides:
        count = lax.axis_size(axis)
        ends = count - 1
        head = lax.slice_in_dim(cells, 0, width, axis=dim)
        tail = lax.slice_in_dim(cells, cells.shape[dim] - width, cells.shape[dim], axis=dim)
        cells = jnp.concatenate(
            [
                lax.ppermute(tail, axis, [(i, (i + 1) % count) for i in range(ends)]),
                cells,
                lax.ppermute(head, axis, [((i + 1) % count, i) for i in range(ends)]),
            ],
            axis=dim,
        )
    return cells


def partner(x, axis, stride):
    return lax.ppermute(x, axis, [(i, i ^ 1 << stride) for i in range(lax.axis_size(axis))])


def fine_rims(field):
    return with_halo(field, (("row", 1), ("col", 2)), 1)


def face_grid(cond_ext):
    left_vals = cond_ext[1:-1, :-1]
    right_vals = cond_ext[1:-1, 1:]
    total_lr = left_vals + right_vals
    across = jnp.where(
        total_lr > 0, 2.0 * (left_vals * right_vals) / jnp.where(total_lr > 0, total_lr, 1.0), 0.0
    )
    upper_vals = cond_ext[:-1, 1:-1]
    lower_vals = cond_ext[1:, 1:-1]
    total_ud = upper_vals + lower_vals
    downward = jnp.where(
        total_ud > 0, 2.0 * (upper_vals * lower_vals) / jnp.where(total_ud > 0, total_ud, 1.0), 0.0
    )
    return (across[:, 1:], across[:, :-1], downward[1:], downward[:-1])


def mat_apply(vector, matrix):
    return lax.dot_general(vector, matrix, (((1,), (1,)), ((), ())), precision=HIGHEST)


def pair_sum(left, right):
    return lax.dot_general(left, right, (((1,), (1,)), ((), ())), precision=HIGHEST)


def left_product(left, right):
    return lax.dot_general(left, right, (((0,), (0,)), ((), ())), precision=HIGHEST)


def presmooth(rhs, apply_fn, diag_row):
    approx = OMEGA_COARSE * rhs / diag_row
    for sweep_index in range(SWEEPS - 1):
        approx = approx + OMEGA_COARSE * (rhs - apply_fn(approx)) / diag_row
    return approx


def postsmooth(rhs, approx, apply_fn, diag_row):
    for sweep_index in range(SWEEPS):
        approx = approx + OMEGA_COARSE * (rhs - apply_fn(approx)) / diag_row
    return approx


def shards(source, guess, conductivity, storage, aggregates, pair_maps):
    members, tile_rows, tile_cols = source.shape
    labels = jnp.arange(NA, dtype=jnp.int32)

    def one_hot(ids):
        return (ids.reshape(1, -1) == labels[:, None]).astype(jnp.float32)

    cond_ext = fine_rims(conductivity[None])[0]
    east_face, west_face, south_face, north_face = face_grid(cond_ext)
    diagonal = storage + east_face + west_face + south_face + north_face

    def apply_fine(field):
        padded = fine_rims(field)
        beside = (
            east_face * padded[:, 1:-1, 2:]
            + west_face * padded[:, 1:-1, :-2]
            + south_face * padded[:, 2:, 1:-1]
            + north_face * padded[:, :-2, 1:-1]
        )
        return diagonal * field - beside

    member_of = one_hot(aggregates)

    def restrict(field):
        return pair_sum(field.reshape(members, -1), member_of)

    def prolong(coarse):
        return jnp.dot(coarse, member_of, precision=HIGHEST).reshape(members, tile_rows, tile_cols)

    col_ids = jnp.arange(tile_cols, dtype=jnp.int32)[None, :]
    row_ids = jnp.arange(tile_rows, dtype=jnp.int32)[:, None]
    inner_east = jnp.where(col_ids < tile_cols - 1, east_face, 0.0).reshape(1, -1)
    inner_south = jnp.where(row_ids < tile_rows - 1, south_face, 0.0).reshape(1, -1)
    right_of = one_hot(jnp.roll(aggregates, -1, axis=1))
    below_of = one_hot(jnp.roll(aggregates, -1, axis=0))
    horizontal = pair_sum(member_of * inner_east, right_of)
    vertical = pair_sum(member_of * inner_south, below_of)
    diag_sums = jnp.dot(member_of, diagonal.reshape(-1), precision=HIGHEST)
    self_block = jnp.diag(diag_sums) - (horizontal + horizontal.T + vertical + vertical.T)

    def level_one(coarse):
        return restrict(apply_fine(prolong(coarse)))

    solution = guess
    for sweep_index in range(SWEEPS):
        solution = solution + OMEGA_FINE * (source - apply_fine(solution)) / diagonal
    leftover = source - apply_fine(solution)
    rhs_list = [restrict(leftover)]
    mat_list = [self_block]
    diag_one = jnp.diagonal(self_block)[None, :]
    sol_list = [presmooth(rhs_list[0], level_one, diag_one)]
    remainder = rhs_list[0] - level_one(sol_list[0])
    col_bits = lax.axis_size("col").bit_length() - 1
    place = lax.axis_index(("row", "col"))
    bit_list = [0, col_bits, 1, col_bits + 1]
    own_maps = []
    for level in range(LEVELS):
        bit = bit_list[level]
        other_mat, other_rhs = partner((mat_list[-1], remainder), ("row", "col"), bit)
        is_upper = place >> bit & 1 == 1
        mat_lo = jnp.where(is_upper, other_mat, mat_list[-1])
        mat_hi = jnp.where(is_upper, mat_list[-1], other_mat)
        rhs_lo = jnp.where(is_upper, other_rhs, remainder)
        rhs_hi = jnp.where(is_upper, remainder, other_rhs)
        chooser = (pair_maps[level, 0, 0][:, None] == labels[None, :]).astype(jnp.float32)
        q_lo = chooser[:NA]
        q_hi = chooser[NA:]
        coarse_mat = left_product(q_lo, jnp.dot(mat_lo, q_lo, precision=HIGHEST)) + left_product(
            q_hi, jnp.dot(mat_hi, q_hi, precision=HIGHEST)
        )
        coarse_rhs = jnp.dot(rhs_lo, q_lo, precision=HIGHEST) + jnp.dot(
            rhs_hi, q_hi, precision=HIGHEST
        )
        own_maps.append(jnp.where(is_upper, q_hi, q_lo))
        mat_list.append(coarse_mat)
        rhs_list.append(coarse_rhs)
        if level < LEVELS - 1:
            diag_row = jnp.diagonal(coarse_mat)[None, :]
            approx = presmooth(coarse_rhs, partial(mat_apply, matrix=coarse_mat), diag_row)
            remainder = coarse_rhs - mat_apply(approx, coarse_mat)
        else:
            factor = jnp.linalg.cholesky(coarse_mat)
            approx = jax.scipy.linalg.cho_solve((factor, True), coarse_rhs.T).T
        sol_list.append(approx)
    for level in reversed(range(LEVELS)):
        updated = sol_list[level] + mat_apply(sol_list[level + 1], own_maps[level])
        if level > 0:
            matrix = mat_list[level]
            updated = postsmooth(
                rhs_list[level],
                updated,
                partial(mat_apply, matrix=matrix),
                jnp.diagonal(matrix)[None, :],
            )
        else:
            updated = postsmooth(rhs_list[0], updated, level_one, diag_one)
        sol_list[level] = updated
    solution = solution + prolong(sol_list[0])
    for sweep_index in range(SWEEPS):
        solution = solution + OMEGA_FINE * (source - apply_fine(solution)) / diagonal
    residual = source - apply_fine(solution)
    return (solution, residual)


def solution(mesh):
    placed = (
        P(None, "row", "col"),
        P(None, "row", "col"),
        P("row", "col"),
        P("row", "col"),
        P("row", "col"),
        P(None, "row", "col", None),
    )
    return jax.shard_map(
        shards,
        mesh=mesh,
        in_specs=placed,
        out_specs=(P(None, "row", "col"), P(None, "row", "col")),
        check_vma=False,
    )
```

profile of v0, /device:TPU:0, one launch (start us, length us, event | category | flops | bytes accessed | tf_op | source)
XLA Modules:
  0.0 389.7 jit_solution(3631761265934117752)
XLA Ops:
  6.6 5.8 %collective-permute-start = (f32[1,1,128]{2,1,0:T(1,128)S(1)}, f32[1,1,128]{2,1,0:T(1,128)S(1)}, u32[]{:S(2)}, u32[]{:S(2)}) collective-permute-start(f32[1,1,128]{2,1,0:T(1,128)S(1)} %get-tuple-element.67), channel_id=1, source_target_pairs={{0,4},{4,8},{8,12},{12,16},{16,20},{20,24},{24,28},{1,5},{5,9},{9,... | collective-permute-start | bytes 1544 | tf_op jit(solution)/shard_map/ppermute | solution.py:26
  16.4 4.5 %collective-permute-start.2 = (f32[1,34,1]{2,1,0:T(8,128)S(1)}, f32[1,34,1]{2,1,0:T(8,128)S(1)}, u32[]{:S(2)}, u32[]{:S(2)}) collective-permute-start(f32[1,34,1]{2,1,0:T(8,128)S(1)} %get-tuple-element.65), channel_id=1, source_target_pairs={{0,1},{1,2},{2,3},{4,5},{5,6},{6,7},{8,9},{9,10},{10,11},{12,13},{... | collective-permute-start | bytes 416 | tf_op jit(solution)/shard_map/ppermute | solution.py:26
  26.2 4.3 %collective-permute-start.7 = (f32[16,34,1]{2,1,0:T(8,128)S(1)}, f32[16,34,1]{2,1,0:T(8,128)S(1)}, u32[]{:S(2)}, u32[]{:S(2)}) collective-permute-start(f32[16,34,1]{2,1,0:T(8,128)S(1)} %get-tuple-element.29), channel_id=1, source_target_pairs={{0,1},{1,2},{2,3},{4,5},{5,6},{6,7},{8,9},{9,10},{10,11},{12,13},{... | collective-permute-start | bytes 6536 | tf_op jit(solution)/shard_map/ppermute | solution.py:26
  31.9 3.9 collective-permute-start.33
  38.6 10.4 %collective-permute-done.6 = f32[16,34,1]{2,1,0:T(8,128)S(1)} collective-permute-done((f32[16,34,1]{2,1,0:T(8,128)S(1)}, f32[16,34,1]{2,1,0:T(8,128)S(1)}, u32[]{:S(2)}, u32[]{:S(2)}) %collective-permute-start.6) | collective-permute-done | bytes 2208 | tf_op jit(solution)/shard_map/ppermute | solution.py:28
  52.1 3.9 collective-permute-done.9
  59.9 5.2 %collective-permute-done.11 = f32[16,34,1]{2,1,0:T(8,128)S(1)} collective-permute-done((f32[16,34,1]{2,1,0:T(8,128)S(1)}, f32[16,34,1]{2,1,0:T(8,128)S(1)}, u32[]{:S(2)}, u32[]{:S(2)}) %collective-permute-start.11) | collective-permute-done | bytes 2208 | tf_op jit(solution)/shard_map/ppermute | solution.py:26
  65.0 7.2 %collective-permute-done.10 = f32[16,34,1]{2,1,0:T(8,128)S(1)} collective-permute-done((f32[16,34,1]{2,1,0:T(8,128)S(1)}, f32[16,34,1]{2,1,0:T(8,128)S(1)}, u32[]{:S(2)}, u32[]{:S(2)}) %collective-permute-start.10) | collective-permute-done | bytes 2208 | tf_op jit(solution)/shard_map/ppermute | solution.py:28
  72.6 3.4 collective-permute-start.12
  88.5 7.3 %collective-permute-done.14 = f32[16,34,1]{2,1,0:T(8,128)S(1)} collective-permute-done((f32[16,34,1]{2,1,0:T(8,128)S(1)}, f32[16,34,1]{2,1,0:T(8,128)S(1)}, u32[]{:S(2)}, u32[]{:S(2)}) %collective-permute-start.14) | collective-permute-done | bytes 2208 | tf_op jit(solution)/shard_map/ppermute | solution.py:28
  96.2 3.4 collective-permute-start.16
  107.4 5.0 %collective-permute-done.19 = f32[16,34,1]{2,1,0:T(8,128)S(1)} collective-permute-done((f32[16,34,1]{2,1,0:T(8,128)S(1)}, f32[16,34,1]{2,1,0:T(8,128)S(1)}, u32[]{:S(2)}, u32[]{:S(2)}) %collective-permute-start.19) | collective-permute-done | bytes 2208 | tf_op jit(solution)/shard_map/ppermute | solution.py:26
  112.4 7.3 %collective-permute-done.18 = f32[16,34,1]{2,1,0:T(8,128)S(1)} collective-permute-done((f32[16,34,1]{2,1,0:T(8,128)S(1)}, f32[16,34,1]{2,1,0:T(8,128)S(1)}, u32[]{:S(2)}, u32[]{:S(2)}) %collective-permute-start.18) | collective-permute-done | bytes 2208 | tf_op jit(solution)/shard_map/ppermute | solution.py:28
  121.3 3.4 collective-permute-start.20
  133.2 4.9 %collective-permute-done.23 = f32[16,34,1]{2,1,0:T(8,128)S(1)} collective-permute-done((f32[16,34,1]{2,1,0:T(8,128)S(1)}, f32[16,34,1]{2,1,0:T(8,128)S(1)}, u32[]{:S(2)}, u32[]{:S(2)}) %collective-permute-start.23) | collective-permute-done | bytes 2208 | tf_op jit(solution)/shard_map/ppermute | solution.py:26
  138.1 8.3 %collective-permute-done.22 = f32[16,34,1]{2,1,0:T(8,128)S(1)} collective-permute-done((f32[16,34,1]{2,1,0:T(8,128)S(1)}, f32[16,34,1]{2,1,0:T(8,128)S(1)}, u32[]{:S(2)}, u32[]{:S(2)}) %collective-permute-start.22) | collective-permute-done | bytes 2208 | tf_op jit(solution)/shard_map/ppermute | solution.py:28
  147.9 3.7 collective-permute-start.24
  153.1 3.8 collective-permute-done.25
  166.0 7.2 %collective-permute-done.26 = f32[16,34,1]{2,1,0:T(8,128)S(1)} collective-permute-done((f32[16,34,1]{2,1,0:T(8,128)S(1)}, f32[16,34,1]{2,1,0:T(8,128)S(1)}, u32[]{:S(2)}, u32[]{:S(2)}) %collective-permute-start.26) | collective-permute-done | bytes 2208 | tf_op jit(solution)/shard_map/ppermute | solution.py:28
  174.7 3.4 collective-permute-start.28
  184.8 5.5 %collective-permute-done.31 = f32[16,34,1]{2,1,0:T(8,128)S(1)} collective-permute-done((f32[16,34,1]{2,1,0:T(8,128)S(1)}, f32[16,34,1]{2,1,0:T(8,128)S(1)}, u32[]{:S(2)}, u32[]{:S(2)}) %collective-permute-start.31) | collective-permute-done | bytes 2208 | tf_op jit(solution)/shard_map/ppermute | solution.py:26
  190.3 7.2 %collective-permute-done.30 = f32[16,34,1]{2,1,0:T(8,128)S(1)} collective-permute-done((f32[16,34,1]{2,1,0:T(8,128)S(1)}, f32[16,34,1]{2,1,0:T(8,128)S(1)}, u32[]{:S(2)}, u32[]{:S(2)}) %collective-permute-start.30) | collective-permute-done | bytes 2208 | tf_op jit(solution)/shard_map/ppermute | solution.py:28
  198.6 5.8 %cholesky.13 = f32[64,64]{1,0:T(8,128)S(1)} custom-call(f32[64,64]{1,0:T(8,128)S(1)} %fusion.250), custom_call_target="Cholesky" | custom-call | tf_op jit(solution)/shard_map/jit(cholesky)/cholesky | solution.py:165
  208.6 3.0 collective-permute-done.36
  213.2 4.9 %custom-call.10 = f32[1,64,64]{1,2,0:T(8,128)S(1)} custom-call(f32[1,64,64]{2,1,0:T(8,128)S(1)} %fusion.240), custom_call_target="InvertDiagBlocksLowerTriangular" | custom-call | tf_op jit(solution)/shard_map/jit(_cho_solve)/triangular_solve | solution.py:166
  224.3 4.0 %collective-permute-done.41 = f32[16,1,128]{2,1,0:T(1,128)S(1)} collective-permute-done((f32[16,1,128]{2,1,0:T(1,128)S(1)}, f32[16,1,128]{2,1,0:T(1,128)S(1)}, u32[]{:S(2)}, u32[]{:S(2)}) %collective-permute-start.41) | collective-permute-done | bytes 8224 | tf_op jit(solution)/shard_map/ppermute | solution.py:28
  228.5 3.7 collective-permute-start.43
  233.5 5.3 %collective-permute-done.43 = f32[16,34,1]{2,1,0:T(8,128)S(1)} collective-permute-done((f32[16,34,1]{2,1,0:T(8,128)S(1)}, f32[16,34,1]{2,1,0:T(8,128)S(1)}, u32[]{:S(2)}, u32[]{:S(2)}) %collective-permute-start.43) | collective-permute-done | bytes 2208 | tf_op jit(solution)/shard_map/ppermute | solution.py:26
  238.8 7.2 %collective-permute-done.42 = f32[16,34,1]{2,1,0:T(8,128)S(1)} collective-permute-done((f32[16,34,1]{2,1,0:T(8,128)S(1)}, f32[16,34,1]{2,1,0:T(8,128)S(1)}, u32[]{:S(2)}, u32[]{:S(2)}) %collective-permute-start.42) | collective-permute-done | bytes 2208 | tf_op jit(solution)/shard_map/ppermute | solution.py:28
  247.6 3.4 collective-permute-start.44
  254.6 3.4 collective-permute-start.47
  259.3 5.3 %collective-permute-done.47 = f32[16,34,1]{2,1,0:T(8,128)S(1)} collective-permute-done((f32[16,34,1]{2,1,0:T(8,128)S(1)}, f32[16,34,1]{2,1,0:T(8,128)S(1)}, u32[]{:S(2)}, u32[]{:S(2)}) %collective-permute-start.47) | collective-permute-done | bytes 2208 | tf_op jit(solution)/shard_map/ppermute | solution.py:26
  264.6 7.2 %collective-permute-done.46 = f32[16,34,1]{2,1,0:T(8,128)S(1)} collective-permute-done((f32[16,34,1]{2,1,0:T(8,128)S(1)}, f32[16,34,1]{2,1,0:T(8,128)S(1)}, u32[]{:S(2)}, u32[]{:S(2)}) %collective-permute-start.46) | collective-permute-done | bytes 2208 | tf_op jit(solution)/shard_map/ppermute | solution.py:28
  273.4 3.4 collective-permute-start.48
  283.8 5.0 %collective-permute-done.51 = f32[16,34,1]{2,1,0:T(8,128)S(1)} collective-permute-done((f32[16,34,1]{2,1,0:T(8,128)S(1)}, f32[16,34,1]{2,1,0:T(8,128)S(1)}, u32[]{:S(2)}, u32[]{:S(2)}) %collective-permute-start.51) | collective-permute-done | bytes 2208 | tf_op jit(solution)/shard_map/ppermute | solution.py:26
  288.7 7.3 %collective-permute-done.50 = f32[16,34,1]{2,1,0:T(8,128)S(1)} collective-permute-done((f32[16,34,1]{2,1,0:T(8,128)S(1)}, f32[16,34,1]{2,1,0:T(8,128)S(1)}, u32[]{:S(2)}, u32[]{:S(2)}) %collective-permute-start.50) | collective-permute-done | bytes 2208 | tf_op jit(solution)/shard_map/ppermute | solution.py:28
  297.7 3.4 collective-permute-start.52
  307.4 5.4 %collective-permute-done.55 = f32[16,34,1]{2,1,0:T(8,128)S(1)} collective-permute-done((f32[16,34,1]{2,1,0:T(8,128)S(1)}, f32[16,34,1]{2,1,0:T(8,128)S(1)}, u32[]{:S(2)}, u32[]{:S(2)}) %collective-permute-start.55) | collective-permute-done | bytes 2208 | tf_op jit(solution)/shard_map/ppermute | solution.py:26
  312.9 7.3 %collective-permute-done.54 = f32[16,34,1]{2,1,0:T(8,128)S(1)} collective-permute-done((f32[16,34,1]{2,1,0:T(8,128)S(1)}, f32[16,34,1]{2,1,0:T(8,128)S(1)}, u32[]{:S(2)}, u32[]{:S(2)}) %collective-permute-start.54) | collective-permute-done | bytes 2208 | tf_op jit(solution)/shard_map/ppermute | solution.py:28
  320.6 3.2 collective-permute-start.56
  330.2 5.8 %collective-permute-done.59 = f32[16,34,1]{2,1,0:T(8,128)S(1)} collective-permute-done((f32[16,34,1]{2,1,0:T(8,128)S(1)}, f32[16,34,1]{2,1,0:T(8,128)S(1)}, u32[]{:S(2)}, u32[]{:S(2)}) %collective-permute-start.59) | collective-permute-done | bytes 2208 | tf_op jit(solution)/shard_map/ppermute | solution.py:26
  336.0 7.2 %collective-permute-done.58 = f32[16,34,1]{2,1,0:T(8,128)S(1)} collective-permute-done((f32[16,34,1]{2,1,0:T(8,128)S(1)}, f32[16,34,1]{2,1,0:T(8,128)S(1)}, u32[]{:S(2)}, u32[]{:S(2)}) %collective-permute-start.58) | collective-permute-done | bytes 2208 | tf_op jit(solution)/shard_map/ppermute | solution.py:28
  343.6 3.0 collective-permute-start.60
  352.9 5.8 %collective-permute-done.63 = f32[16,34,1]{2,1,0:T(8,128)S(1)} collective-permute-done((f32[16,34,1]{2,1,0:T(8,128)S(1)}, f32[16,34,1]{2,1,0:T(8,128)S(1)}, u32[]{:S(2)}, u32[]{:S(2)}) %collective-permute-start.63) | collective-permute-done | bytes 2208 | tf_op jit(solution)/shard_map/ppermute | solution.py:26
  358.7 7.2 %collective-permute-done.62 = f32[16,34,1]{2,1,0:T(8,128)S(1)} collective-permute-done((f32[16,34,1]{2,1,0:T(8,128)S(1)}, f32[16,34,1]{2,1,0:T(8,128)S(1)}, u32[]{:S(2)}, u32[]{:S(2)}) %collective-permute-start.62) | collective-permute-done | bytes 2208 | tf_op jit(solution)/shard_map/ppermute | solution.py:28
  366.3 3.0 collective-permute-start.64
  375.6 5.8 %collective-permute-done.67 = f32[16,34,1]{2,1,0:T(8,128)S(1)} collective-permute-done((f32[16,34,1]{2,1,0:T(8,128)S(1)}, f32[16,34,1]{2,1,0:T(8,128)S(1)}, u32[]{:S(2)}, u32[]{:S(2)}) %collective-permute-start.67) | collective-permute-done | bytes 2208 | tf_op jit(solution)/shard_map/ppermute | solution.py:26
  381.4 7.2 %collective-permute-done.66 = f32[16,34,1]{2,1,0:T(8,128)S(1)} collective-permute-done((f32[16,34,1]{2,1,0:T(8,128)S(1)}, f32[16,34,1]{2,1,0:T(8,128)S(1)}, u32[]{:S(2)}, u32[]{:S(2)}) %collective-permute-start.66) | collective-permute-done | bytes 2208 | tf_op jit(solution)/shard_map/ppermute | solution.py:28
  (268 shorter events, 135.0 us)
Async XLA Ops:
  1.5 24.3 %collective-permute-start.4 = (f32[16,1,128]{2,1,0:T(1,128)S(1)}, f32[16,1,128]{2,1,0:T(1,128)S(1)}, u32[]{:S(2)}, u32[]{:S(2)}) collective-permute-start(f32[16,1,128]{2,1,0:T(1,128)S(1)} %get-tuple-element.57), channel_id=1, source_target_pairs={{0,4},{4,8},{8,12},{12,16},{16,20},{20,24},{24,28},{1,5},{5,9},{9,... | collective-permute-start | bytes 24584 | tf_op jit(solution)/shard_map/ppermute | solution.py:26
  4.0 21.9 %collective-permute-start.5 = (f32[16,1,128]{2,1,0:T(1,128)S(1)}, f32[16,1,128]{2,1,0:T(1,128)S(1)}, u32[]{:S(2)}, u32[]{:S(2)}) collective-permute-start(f32[16,1,128]{2,1,0:T(1,128)S(1)} %get-tuple-element.56), channel_id=1, source_target_pairs={{4,0},{8,4},{12,8},{16,12},{20,16},{24,20},{28,24},{5,1},{9,5},{13... | collective-permute-start | bytes 24584 | tf_op jit(solution)/shard_map/ppermute | solution.py:28
  5.3 9.7 %collective-permute-start.1 = (f32[1,1,128]{2,1,0:T(1,128)S(1)}, f32[1,1,128]{2,1,0:T(1,128)S(1)}, u32[]{:S(2)}, u32[]{:S(2)}) collective-permute-start(f32[1,1,128]{2,1,0:T(1,128)S(1)} %get-tuple-element.68), channel_id=1, source_target_pairs={{4,0},{8,4},{12,8},{16,12},{20,16},{24,20},{28,24},{5,1},{9,5},{13... | collective-permute-start | bytes 1544 | tf_op jit(solution)/shard_map/ppermute | solution.py:28
  6.6 8.4 %collective-permute-start = (f32[1,1,128]{2,1,0:T(1,128)S(1)}, f32[1,1,128]{2,1,0:T(1,128)S(1)}, u32[]{:S(2)}, u32[]{:S(2)}) collective-permute-start(f32[1,1,128]{2,1,0:T(1,128)S(1)} %get-tuple-element.67), channel_id=1, source_target_pairs={{0,4},{4,8},{8,12},{12,16},{16,20},{20,24},{24,28},{1,5},{5,9},{9,... | collective-permute-start | bytes 1544 | tf_op jit(solution)/shard_map/ppermute | solution.py:26
  15.1 5.8 %collective-permute-start.3 = (f32[1,34,1]{2,1,0:T(8,128)S(1)}, f32[1,34,1]{2,1,0:T(8,128)S(1)}, u32[]{:S(2)}, u32[]{:S(2)}) collective-permute-start(f32[1,34,1]{2,1,0:T(8,128)S(1)} %get-tuple-element.66), channel_id=1, source_target_pairs={{1,0},{2,1},{3,2},{5,4},{6,5},{7,6},{9,8},{10,9},{11,10},{13,12},{... | collective-permute-start | bytes 416 | tf_op jit(solution)/shard_map/ppermute | solution.py:28
  16.4 6.0 %collective-permute-start.2 = (f32[1,34,1]{2,1,0:T(8,128)S(1)}, f32[1,34,1]{2,1,0:T(8,128)S(1)}, u32[]{:S(2)}, u32[]{:S(2)}) collective-permute-start(f32[1,34,1]{2,1,0:T(8,128)S(1)} %get-tuple-element.65), channel_id=1, source_target_pairs={{0,1},{1,2},{2,3},{4,5},{5,6},{6,7},{8,9},{9,10},{10,11},{12,13},{... | collective-permute-start | bytes 416 | tf_op jit(solution)/shard_map/ppermute | solution.py:26
  26.2 12.4 %collective-permute-start.7 = (f32[16,34,1]{2,1,0:T(8,128)S(1)}, f32[16,34,1]{2,1,0:T(8,128)S(1)}, u32[]{:S(2)}, u32[]{:S(2)}) collective-permute-start(f32[16,34,1]{2,1,0:T(8,128)S(1)} %get-tuple-element.29), channel_id=1, source_target_pairs={{0,1},{1,2},{2,3},{4,5},{5,6},{6,7},{8,9},{9,10},{10,11},{12,13},{... | collective-permute-start | bytes 6536 | tf_op jit(solution)/shard_map/ppermute | solution.py:26
  30.5 18.4 %collective-permute-start.6 = (f32[16,34,1]{2,1,0:T(8,128)S(1)}, f32[16,34,1]{2,1,0:T(8,128)S(1)}, u32[]{:S(2)}, u32[]{:S(2)}) collective-permute-start(f32[16,34,1]{2,1,0:T(8,128)S(1)} %get-tuple-element.28), channel_id=1, source_target_pairs={{1,0},{2,1},{3,2},{5,4},{6,5},{7,6},{9,8},{10,9},{11,10},{13,12},{... | collective-permute-start | bytes 6536 | tf_op jit(solution)/shard_map/ppermute | solution.py:28
  31.9 20.0 %collective-permute-start.33 = (f32[64,64]{1,0:T(8,128)S(1)}, f32[64,64]{1,0:T(8,128)S(1)}, u32[]{:S(2)}, u32[]{:S(2)}) collective-permute-start(f32[64,64]{1,0:T(8,128)S(1)} %fusion.251), channel_id=1, source_target_pairs={{0,1},{1,0},{2,3},{3,2},{4,5},{5,4},{6,7},{7,6},{8,9},{9,8},{10,11... | collective-permute-start | bytes 49160 | tf_op jit(solution)/shard_map/ppermute | solution.py:36
  50.6 5.3 %collective-permute-start.9 = (f32[16,1,128]{2,1,0:T(1,128)S(1)}, f32[16,1,128]{2,1,0:T(1,128)S(1)}, u32[]{:S(2)}, u32[]{:S(2)}) collective-permute-start(f32[16,1,128]{2,1,0:T(1,128)S(1)} %get-tuple-element.54), channel_id=1, source_target_pairs={{4,0},{8,4},{12,8},{16,12},{20,16},{24,20},{28,24},{5,1},{9,5},{13... | collective-permute-start | bytes 24584 | tf_op jit(solution)/shard_map/ppermute | solution.py:28
  56.2 8.9 %collective-permute-start.11 = (f32[16,34,1]{2,1,0:T(8,128)S(1)}, f32[16,34,1]{2,1,0:T(8,128)S(1)}, u32[]{:S(2)}, u32[]{:S(2)}) collective-permute-start(f32[16,34,1]{2,1,0:T(8,128)S(1)} %get-tuple-element.27), channel_id=1, source_target_pairs={{0,1},{1,2},{2,3},{4,5},{5,6},{6,7},{8,9},{9,10},{10,11},{12,13},{... | collective-permute-start | bytes 6536 | tf_op jit(solution)/shard_map/ppermute | solution.py:26
  58.4 13.8 %collective-permute-start.10 = (f32[16,34,1]{2,1,0:T(8,128)S(1)}, f32[16,34,1]{2,1,0:T(8,128)S(1)}, u32[]{:S(2)}, u32[]{:S(2)}) collective-permute-start(f32[16,34,1]{2,1,0:T(8,128)S(1)} %get-tuple-element.26), channel_id=1, source_target_pairs={{1,0},{2,1},{3,2},{5,4},{6,5},{7,6},{9,8},{10,9},{11,10},{13,12},{... | collective-permute-start | bytes 6536 | tf_op jit(solution)/shard_map/ppermute | solution.py:28
  80.5 8.0 %collective-permute-start.15 = (f32[16,34,1]{2,1,0:T(8,128)S(1)}, f32[16,34,1]{2,1,0:T(8,128)S(1)}, u32[]{:S(2)}, u32[]{:S(2)}) collective-permute-start(f32[16,34,1]{2,1,0:T(8,128)S(1)} %get-tuple-element.25), channel_id=1, source_target_pairs={{0,1},{1,2},{2,3},{4,5},{5,6},{6,7},{8,9},{9,10},{10,11},{12,13},{... | collective-permute-start | bytes 6536 | tf_op jit(solution)/shard_map/ppermute | solution.py:26
  82.0 13.8 %collective-permute-start.14 = (f32[16,34,1]{2,1,0:T(8,128)S(1)}, f32[16,34,1]{2,1,0:T(8,128)S(1)}, u32[]{:S(2)}, u32[]{:S(2)}) collective-permute-start(f32[16,34,1]{2,1,0:T(8,128)S(1)} %get-tuple-element.24), channel_id=1, source_target_pairs={{1,0},{2,1},{3,2},{5,4},{6,5},{7,6},{9,8},{10,9},{11,10},{13,12},{... | collective-permute-start | bytes 6536 | tf_op jit(solution)/shard_map/ppermute | solution.py:28
  84.3 16.6 %collective-permute-start.35 = (f32[64,64]{1,0:T(8,128)S(1)}, f32[64,64]{1,0:T(8,128)S(1)}, u32[]{:S(2)}, u32[]{:S(2)}) collective-permute-start(f32[64,64]{1,0:T(8,128)S(1)} %convolution_add_fusion.3), channel_id=1, source_target_pairs={{0,4},{1,5},{2,6},{3,7},{4,0},{5,1},{6,2},{7,3},{8,12},{9,13},{10,... | collective-permute-start | bytes 49160 | tf_op jit(solution)/shard_map/ppermute | solution.py:36
  96.2 5.1 %collective-permute-start.16 = (f32[16,1,128]{2,1,0:T(1,128)S(1)}, f32[16,1,128]{2,1,0:T(1,128)S(1)}, u32[]{:S(2)}, u32[]{:S(2)}) collective-permute-start(f32[16,1,128]{2,1,0:T(1,128)S(1)} %get-tuple-element.51), channel_id=1, source_target_pairs={{0,4},{4,8},{8,12},{12,16},{16,20},{20,24},{24,28},{1,5},{5,9},{9,... | collective-permute-start | bytes 24584 | tf_op jit(solution)/shard_map/ppermute | solution.py:26
  104.4 8.0 %collective-permute-start.19 = (f32[16,34,1]{2,1,0:T(8,128)S(1)}, f32[16,34,1]{2,1,0:T(8,128)S(1)}, u32[]{:S(2)}, u32[]{:S(2)}) collective-permute-start(f32[16,34,1]{2,1,0:T(8,128)S(1)} %get-tuple-element.23), channel_id=1, source_target_pairs={{0,1},{1,2},{2,3},{4,5},{5,6},{6,7},{8,9},{9,10},{10,11},{12,13},{... | collective-permute-start | bytes 6536 | tf_op jit(solution)/shard_map/ppermute | solution.py:26
  105.9 13.8 %collective-permute-start.18 = (f32[16,34,1]{2,1,0:T(8,128)S(1)}, f32[16,34,1]{2,1,0:T(8,128)S(1)}, u32[]{:S(2)}, u32[]{:S(2)}) collective-permute-start(f32[16,34,1]{2,1,0:T(8,128)S(1)} %get-tuple-element.22), channel_id=1, source_target_pairs={{1,0},{2,1},{3,2},{5,4},{6,5},{7,6},{9,8},{10,9},{11,10},{13,12},{... | collective-permute-start | bytes 6536 | tf_op jit(solution)/shard_map/ppermute | solution.py:28
  121.3 5.8 %collective-permute-start.20 = (f32[16,1,128]{2,1,0:T(1,128)S(1)}, f32[16,1,128]{2,1,0:T(1,128)S(1)}, u32[]{:S(2)}, u32[]{:S(2)}) collective-permute-start(f32[16,1,128]{2,1,0:T(1,128)S(1)} %get-tuple-element.49), channel_id=1, source_target_pairs={{0,4},{4,8},{8,12},{12,16},{16,20},{20,24},{24,28},{1,5},{5,9},{9,... | collective-permute-start | bytes 24584 | tf_op jit(solution)/shard_map/ppermute | solution.py:26
  124.8 5.2 %collective-permute-start.21 = (f32[16,1,128]{2,1,0:T(1,128)S(1)}, f32[16,1,128]{2,1,0:T(1,128)S(1)}, u32[]{:S(2)}, u32[]{:S(2)}) collective-permute-start(f32[16,1,128]{2,1,0:T(1,128)S(1)} %get-tuple-element.48), channel_id=1, source_target_pairs={{4,0},{8,4},{12,8},{16,12},{20,16},{24,20},{28,24},{5,1},{9,5},{13... | collective-permute-start | bytes 24584 | tf_op jit(solution)/shard_map/ppermute | solution.py:28
  127.1 5.8 %collective-permute-start.37 = (f32[64,64]{1,0:T(8,128)S(1)}, f32[64,64]{1,0:T(8,128)S(1)}, u32[]{:S(2)}, u32[]{:S(2)}) collective-permute-start(f32[64,64]{1,0:T(8,128)S(1)} %convolution_add_fusion.2), channel_id=1, source_target_pairs={{0,2},{1,3},{2,0},{3,1},{4,6},{5,7},{6,4},{7,5},{8,10},{9,11},{10,... | collective-permute-start | bytes 49160 | tf_op jit(solution)/shard_map/ppermute | solution.py:36
  130.1 8.0 %collective-permute-start.23 = (f32[16,34,1]{2,1,0:T(8,128)S(1)}, f32[16,34,1]{2,1,0:T(8,128)S(1)}, u32[]{:S(2)}, u32[]{:S(2)}) collective-permute-start(f32[16,34,1]{2,1,0:T(8,128)S(1)} %get-tuple-element.21), channel_id=1, source_target_pairs={{0,1},{1,2},{2,3},{4,5},{5,6},{6,7},{8,9},{9,10},{10,11},{12,13},{... | collective-permute-start | bytes 6536 | tf_op jit(solution)/shard_map/ppermute | solution.py:26
  131.6 14.8 %collective-permute-start.22 = (f32[16,34,1]{2,1,0:T(8,128)S(1)}, f32[16,34,1]{2,1,0:T(8,128)S(1)}, u32[]{:S(2)}, u32[]{:S(2)}) collective-permute-start(f32[16,34,1]{2,1,0:T(8,128)S(1)} %get-tuple-element.20), channel_id=1, source_target_pairs={{1,0},{2,1},{3,2},{5,4},{6,5},{7,6},{9,8},{10,9},{11,10},{13,12},{... | collective-permute-start | bytes 6536 | tf_op jit(solution)/shard_map/ppermute | solution.py:28
  147.9 5.2 %collective-permute-start.24 = (f32[16,1,128]{2,1,0:T(1,128)S(1)}, f32[16,1,128]{2,1,0:T(1,128)S(1)}, u32[]{:S(2)}, u32[]{:S(2)}) collective-permute-start(f32[16,1,128]{2,1,0:T(1,128)S(1)} %get-tuple-element.47), channel_id=1, source_target_pairs={{0,4},{4,8},{8,12},{12,16},{16,20},{20,24},{24,28},{1,5},{5,9},{9,... | collective-permute-start | bytes 24584 | tf_op jit(solution)/shard_map/ppermute | solution.py:26
  151.6 5.3 %collective-permute-start.25 = (f32[16,1,128]{2,1,0:T(1,128)S(1)}, f32[16,1,128]{2,1,0:T(1,128)S(1)}, u32[]{:S(2)}, u32[]{:S(2)}) collective-permute-start(f32[16,1,128]{2,1,0:T(1,128)S(1)} %get-tuple-element.46), channel_id=1, source_target_pairs={{4,0},{8,4},{12,8},{16,12},{20,16},{24,20},{28,24},{5,1},{9,5},{13... | collective-permute-start | bytes 24584 | tf_op jit(solution)/shard_map/ppermute | solution.py:28
  157.1 8.9 %collective-permute-start.27 = (f32[16,34,1]{2,1,0:T(8,128)S(1)}, f32[16,34,1]{2,1,0:T(8,128)S(1)}, u32[]{:S(2)}, u32[]{:S(2)}) collective-permute-start(f32[16,34,1]{2,1,0:T(8,128)S(1)} %get-tuple-element.19), channel_id=1, source_target_pairs={{0,1},{1,2},{2,3},{4,5},{5,6},{6,7},{8,9},{9,10},{10,11},{12,13},{... | collective-permute-start | bytes 6536 | tf_op jit(solution)/shard_map/ppermute | solution.py:26
  159.3 13.8 %collective-permute-start.26 = (f32[16,34,1]{2,1,0:T(8,128)S(1)}, f32[16,34,1]{2,1,0:T(8,128)S(1)}, u32[]{:S(2)}, u32[]{:S(2)}) collective-permute-start(f32[16,34,1]{2,1,0:T(8,128)S(1)} %get-tuple-element.18), channel_id=1, source_target_pairs={{1,0},{2,1},{3,2},{5,4},{6,5},{7,6},{9,8},{10,9},{11,10},{13,12},{... | collective-permute-start | bytes 6536 | tf_op jit(solution)/shard_map/ppermute | solution.py:28
  161.9 17.6 %collective-permute-start.38 = (f32[64,64]{1,0:T(8,128)S(1)}, f32[64,64]{1,0:T(8,128)S(1)}, u32[]{:S(2)}, u32[]{:S(2)}) collective-permute-start(f32[64,64]{1,0:T(8,128)S(1)} %convolution_add_fusion.1), channel_id=1, source_target_pairs={{0,8},{1,9},{2,10},{3,11},{4,12},{5,13},{6,14},{7,15},{8,0},{9,1},... | collective-permute-start | bytes 49160 | tf_op jit(solution)/shard_map/ppermute | solution.py:36
  174.7 5.3 %collective-permute-start.28 = (f32[16,1,128]{2,1,0:T(1,128)S(1)}, f32[16,1,128]{2,1,0:T(1,128)S(1)}, u32[]{:S(2)}, u32[]{:S(2)}) collective-permute-start(f32[16,1,128]{2,1,0:T(1,128)S(1)} %get-tuple-element.45), channel_id=1, source_target_pairs={{0,4},{4,8},{8,12},{12,16},{16,20},{20,24},{24,28},{1,5},{5,9},{9,... | collective-permute-start | bytes 24584 | tf_op jit(solution)/shard_map/ppermute | solution.py:26
  181.4 8.9 %collective-permute-start.31 = (f32[16,34,1]{2,1,0:T(8,128)S(1)}, f32[16,34,1]{2,1,0:T(8,128)S(1)}, u32[]{:S(2)}, u32[]{:S(2)}) collective-permute-start(f32[16,34,1]{2,1,0:T(8,128)S(1)} %get-tuple-element.17), channel_id=1, source_target_pairs={{0,1},{1,2},{2,3},{4,5},{5,6},{6,7},{8,9},{9,10},{10,11},{12,13},{... | collective-permute-start | bytes 6536 | tf_op jit(solution)/shard_map/ppermute | solution.py:26
  183.2 14.3 %collective-permute-start.30 = (f32[16,34,1]{2,1,0:T(8,128)S(1)}, f32[16,34,1]{2,1,0:T(8,128)S(1)}, u32[]{:S(2)}, u32[]{:S(2)}) collective-permute-start(f32[16,34,1]{2,1,0:T(8,128)S(1)} %get-tuple-element.16), channel_id=1, source_target_pairs={{1,0},{2,1},{3,2},{5,4},{6,5},{7,6},{9,8},{10,9},{11,10},{13,12},{... | collective-permute-start | bytes 6536 | tf_op jit(solution)/shard_map/ppermute | solution.py:28
  198.5 5.9 %collective-permute-start.32 = (f32[16,64]{1,0:T(8,128)S(1)}, f32[16,64]{1,0:T(8,128)S(1)}, u32[]{:S(2)}, u32[]{:S(2)}) collective-permute-start(f32[16,64]{1,0:T(8,128)S(1)} %convolution_subtract_fusion.21), channel_id=1, source_target_pairs={{0,1},{1,0},{2,3},{3,2},{4,5},{5,4},{6,7},{7,6},{8,9},{9,8},{10,11... | collective-permute-start | bytes 12296 | tf_op jit(solution)/shard_map/ppermute | solution.py:36
  212.4 5.6 %collective-permute-start.39 = (f32[16,64]{1,0:T(8,128)S(1)}, f32[16,64]{1,0:T(8,128)S(1)}, u32[]{:S(2)}, u32[]{:S(2)}) collective-permute-start(f32[16,64]{1,0:T(8,128)S(1)} %convolution_subtract_fusion.9), channel_id=1, source_target_pairs={{0,8},{1,9},{2,10},{3,11},{4,12},{5,13},{6,14},{7,15},{8,0},{9,1},... | collective-permute-start | bytes 12296 | tf_op jit(solution)/shard_map/ppermute | solution.py:36
  223.0 5.3 %collective-permute-start.41 = (f32[16,1,128]{2,1,0:T(1,128)S(1)}, f32[16,1,128]{2,1,0:T(1,128)S(1)}, u32[]{:S(2)}, u32[]{:S(2)}) collective-permute-start(f32[16,1,128]{2,1,0:T(1,128)S(1)} %get-tuple-element.42), channel_id=1, source_target_pairs={{4,0},{8,4},{12,8},{16,12},{20,16},{24,20},{28,24},{5,1},{9,5},{13... | collective-permute-start | bytes 24584 | tf_op jit(solution)/shard_map/ppermute | solution.py:28
  228.5 10.3 %collective-permute-start.43 = (f32[16,34,1]{2,1,0:T(8,128)S(1)}, f32[16,34,1]{2,1,0:T(8,128)S(1)}, u32[]{:S(2)}, u32[]{:S(2)}) collective-permute-start(f32[16,34,1]{2,1,0:T(8,128)S(1)} %get-tuple-element.15), channel_id=1, source_target_pairs={{0,1},{1,2},{2,3},{4,5},{5,6},{6,7},{8,9},{9,10},{10,11},{12,13},{... | collective-permute-start | bytes 6536 | tf_op jit(solution)/shard_map/ppermute | solution.py:26
  232.2 13.8 %collective-permute-start.42 = (f32[16,34,1]{2,1,0:T(8,128)S(1)}, f32[16,34,1]{2,1,0:T(8,128)S(1)}, u32[]{:S(2)}, u32[]{:S(2)}) collective-permute-start(f32[16,34,1]{2,1,0:T(8,128)S(1)} %get-tuple-element.14), channel_id=1, source_target_pairs={{1,0},{2,1},{3,2},{5,4},{6,5},{7,6},{9,8},{10,9},{11,10},{13,12},{... | collective-permute-start | bytes 6536 | tf_op jit(solution)/shard_map/ppermute | solution.py:28
  254.6 10.0 %collective-permute-start.47 = (f32[16,34,1]{2,1,0:T(8,128)S(1)}, f32[16,34,1]{2,1,0:T(8,128)S(1)}, u32[]{:S(2)}, u32[]{:S(2)}) collective-permute-start(f32[16,34,1]{2,1,0:T(8,128)S(1)} %get-tuple-element.13), channel_id=1, source_target_pairs={{0,1},{1,2},{2,3},{4,5},{5,6},{6,7},{8,9},{9,10},{10,11},{12,13},{... | collective-permute-start | bytes 6536 | tf_op jit(solution)/shard_map/ppermute | solution.py:26
  258.0 13.8 %collective-permute-start.46 = (f32[16,34,1]{2,1,0:T(8,128)S(1)}, f32[16,34,1]{2,1,0:T(8,128)S(1)}, u32[]{:S(2)}, u32[]{:S(2)}) collective-permute-start(f32[16,34,1]{2,1,0:T(8,128)S(1)} %get-tuple-element.12), channel_id=1, source_target_pairs={{1,0},{2,1},{3,2},{5,4},{6,5},{7,6},{9,8},{10,9},{11,10},{13,12},{... | collective-permute-start | bytes 6536 | tf_op jit(solution)/shard_map/ppermute | solution.py:28
  280.8 8.0 %collective-permute-start.51 = (f32[16,34,1]{2,1,0:T(8,128)S(1)}, f32[16,34,1]{2,1,0:T(8,128)S(1)}, u32[]{:S(2)}, u32[]{:S(2)}) collective-permute-start(f32[16,34,1]{2,1,0:T(8,128)S(1)} %get-tuple-element.11), channel_id=1, source_target_pairs={{0,1},{1,2},{2,3},{4,5},{5,6},{6,7},{8,9},{9,10},{10,11},{12,13},{... | collective-permute-start | bytes 6536 | tf_op jit(solution)/shard_map/ppermute | solution.py:26
  282.2 13.8 %collective-permute-start.50 = (f32[16,34,1]{2,1,0:T(8,128)S(1)}, f32[16,34,1]{2,1,0:T(8,128)S(1)}, u32[]{:S(2)}, u32[]{:S(2)}) collective-permute-start(f32[16,34,1]{2,1,0:T(8,128)S(1)} %get-tuple-element.10), channel_id=1, source_target_pairs={{1,0},{2,1},{3,2},{5,4},{6,5},{7,6},{9,8},{10,9},{11,10},{13,12},{... | collective-permute-start | bytes 6536 | tf_op jit(solution)/shard_map/ppermute | solution.py:28
  304.4 8.4 %collective-permute-start.55 = (f32[16,34,1]{2,1,0:T(8,128)S(1)}, f32[16,34,1]{2,1,0:T(8,128)S(1)}, u32[]{:S(2)}, u32[]{:S(2)}) collective-permute-start(f32[16,34,1]{2,1,0:T(8,128)S(1)} %get-tuple-element.9), channel_id=1, source_target_pairs={{0,1},{1,2},{2,3},{4,5},{5,6},{6,7},{8,9},{9,10},{10,11},{12,13},{... | collective-permute-start | bytes 6536 | tf_op jit(solution)/shard_map/ppermute | solution.py:26
  306.1 14.1 %collective-permute-start.54 = (f32[16,34,1]{2,1,0:T(8,128)S(1)}, f32[16,34,1]{2,1,0:T(8,128)S(1)}, u32[]{:S(2)}, u32[]{:S(2)}) collective-permute-start(f32[16,34,1]{2,1,0:T(8,128)S(1)} %get-tuple-element.8), channel_id=1, source_target_pairs={{1,0},{2,1},{3,2},{5,4},{6,5},{7,6},{9,8},{10,9},{11,10},{13,12},{... | collective-permute-start | bytes 6536 | tf_op jit(solution)/shard_map/ppermute | solution.py:28
  327.1 8.9 %collective-permute-start.59 = (f32[16,34,1]{2,1,0:T(8,128)S(1)}, f32[16,34,1]{2,1,0:T(8,128)S(1)}, u32[]{:S(2)}, u32[]{:S(2)}) collective-permute-start(f32[16,34,1]{2,1,0:T(8,128)S(1)} %get-tuple-element.7), channel_id=1, source_target_pairs={{0,1},{1,2},{2,3},{4,5},{5,6},{6,7},{8,9},{9,10},{10,11},{12,13},{... | collective-permute-start | bytes 6536 | tf_op jit(solution)/shard_map/ppermute | solution.py:26
  328.9 14.3 %collective-permute-start.58 = (f32[16,34,1]{2,1,0:T(8,128)S(1)}, f32[16,34,1]{2,1,0:T(8,128)S(1)}, u32[]{:S(2)}, u32[]{:S(2)}) collective-permute-start(f32[16,34,1]{2,1,0:T(8,128)S(1)} %get-tuple-element.6), channel_id=1, source_target_pairs={{1,0},{2,1},{3,2},{5,4},{6,5},{7,6},{9,8},{10,9},{11,10},{13,12},{... | collective-permute-start | bytes 6536 | tf_op jit(solution)/shard_map/ppermute | solution.py:28
  349.8 8.9 %collective-permute-start.63 = (f32[16,34,1]{2,1,0:T(8,128)S(1)}, f32[16,34,1]{2,1,0:T(8,128)S(1)}, u32[]{:S(2)}, u32[]{:S(2)}) collective-permute-start(f32[16,34,1]{2,1,0:T(8,128)S(1)} %get-tuple-element.5), channel_id=1, source_target_pairs={{0,1},{1,2},{2,3},{4,5},{5,6},{6,7},{8,9},{9,10},{10,11},{12,13},{... | collective-permute-start | bytes 6536 | tf_op jit(solution)/shard_map/ppermute | solution.py:26
  351.6 14.3 %collective-permute-start.62 = (f32[16,34,1]{2,1,0:T(8,128)S(1)}, f32[16,34,1]{2,1,0:T(8,128)S(1)}, u32[]{:S(2)}, u32[]{:S(2)}) collective-permute-start(f32[16,34,1]{2,1,0:T(8,128)S(1)} %get-tuple-element.4), channel_id=1, source_target_pairs={{1,0},{2,1},{3,2},{5,4},{6,5},{7,6},{9,8},{10,9},{11,10},{13,12},{... | collective-permute-start | bytes 6536 | tf_op jit(solution)/shard_map/ppermute | solution.py:28
  372.5 8.9 %collective-permute-start.67 = (f32[16,34,1]{2,1,0:T(8,128)S(1)}, f32[16,34,1]{2,1,0:T(8,128)S(1)}, u32[]{:S(2)}, u32[]{:S(2)}) collective-permute-start(f32[16,34,1]{2,1,0:T(8,128)S(1)} %get-tuple-element.3), channel_id=1, source_target_pairs={{0,1},{1,2},{2,3},{4,5},{5,6},{6,7},{8,9},{9,10},{10,11},{12,13},{... | collective-permute-start | bytes 6536 | tf_op jit(solution)/shard_map/ppermute | solution.py:26
  374.3 14.3 %collective-permute-start.66 = (f32[16,34,1]{2,1,0:T(8,128)S(1)}, f32[16,34,1]{2,1,0:T(8,128)S(1)}, u32[]{:S(2)}, u32[]{:S(2)}) collective-permute-start(f32[16,34,1]{2,1,0:T(8,128)S(1)} %get-tuple-element.2), channel_id=1, source_target_pairs={{1,0},{2,1},{3,2},{5,4},{6,5},{7,6},{9,8},{10,9},{11,10},{13,12},{... | collective-permute-start | bytes 6536 | tf_op jit(solution)/shard_map/ppermute | solution.py:28
  (29 other events, 133.3 us)
where the time goes:
time: 392 us; the launch traced here: 390 us
  waiting for transfers between devices  209 us (53%)
  starting transfers between devices  132 us (34%)
  other arithmetic  19 us (5%)
  matrix products  18.5 us (5%)
  local copies, waits for them, and re-layouts  10 us (3%)
    ppermute x30, waiting for transfers between devices, with_halo(): lax.ppermute(head, axis, [((i + 1) % count, i) for i in range(ends)])  138 us
    ppermute x30, starting transfers between devices, with_halo(): lax.ppermute(tail, axis, [(i, (i + 1) % count) for i in range(ends)])  82.6 us
    ppermute x30, waiting for transfers between devices, with_halo(): lax.ppermute(tail, axis, [(i, (i + 1) % count) for i in range(ends)])  66.2 us
    ppermute x30, starting transfers between devices, with_halo(): lax.ppermute(head, axis, [((i + 1) % count, i) for i in range(ends)])  39.2 us
    ppermute x8, starting transfers between devices, partner(): lax.ppermute(x, axis, [(i, i ^ 1 << stride) for i in range(lax.axis_size(...  9.74 us
  transfers between devices with their start and end apart: 68, of which 44 were waited for; matrix products, arithmetic and copies ran while one was open for 6% of the time, Pallas kernels for 0%

commit v1 on v0

v1 whole, which is shorter than its diff:
```python
import functools

import jax
import jax.numpy as jnp
from jax import lax
from jax.experimental import pallas as pl
from jax.experimental.pallas import tpu as pltpu
from jax.sharding import PartitionSpec as P

NA = 64
SWEEPS = 3
LEVELS = 4
OMEGA_FINE = 0.8
OMEGA_COARSE = 0.6
F32 = jnp.float32
BF16 = jnp.bfloat16
MESH = pl.DeviceIdType.MESH
OPP = (1, 0, 3, 2)
NU = 2 * (SWEEPS + 1)
NX0 = 2 * SWEEPS
NN = (((1,), (0,)), ((), ()))
NT = (((1,), (1,)), ((), ()))


def dg(a, b, dims):
    return lax.dot_general(a, b, dims, preferred_element_type=F32)


def split2(x):
    hi = x.astype(BF16)
    return hi, (x - hi.astype(F32)).astype(BF16)


def split3(x):
    hi = x.astype(BF16)
    rest = x - hi.astype(F32)
    mid = rest.astype(BF16)
    return hi, mid, (rest - mid.astype(F32)).astype(BF16)


def dot_parts(x, w_hi, w_lo):
    hi, lo = split2(x)
    return dg(hi, w_hi, NN) + (dg(lo, w_hi, NN) + dg(hi, w_lo, NN))


def dot_hot(x, hot, dims):
    hi, mid, lo = split3(x)
    return dg(hi, hot, dims) + (dg(mid, hot, dims) + dg(lo, hot, dims))


def hot_dot(hot, x, dims):
    hi, mid, lo = split3(x)
    return dg(hot, hi, dims) + (dg(hot, mid, dims) + dg(hot, lo, dims))


def kernel(n_row, n_col, src, guess, cond, sto, agg, pm, sol, res,
           u, left, mo, gmat, rlhs, xt, crecv, arecv, rowbuf, colbuf, rsend, csend,
           xsend, xrecv, msend, mrecv, vsend, vrecv, wmat, bsp, qts, ssem, rsem):
    members, rows, cols = guess.shape
    row = lax.axis_index("row")
    col = lax.axis_index("col")
    has = (row > 0, row < n_row - 1, col > 0, col < n_col - 1)
    dev = ((row - 1, col), (row + 1, col), (row, col - 1), (row, col + 1))
    col_bit = col % 2
    row_bit = row % 2
    col_bit2 = col // 2 % 2
    row_bit2 = row // 2 % 2
    upper = (col_bit, row_bit, col_bit2, row_bit2)
    partner = (
        (row, col + 1 - 2 * col_bit),
        (row + 1 - 2 * row_bit, col),
        (row, col + 2 - 4 * col_bit2),
        (row + 2 - 4 * row_bit2, col),
    )

    barrier = pltpu.get_barrier_semaphore()
    count = jnp.int32(2)
    for d in range(4):
        count = count + has[d].astype(jnp.int32)

        @pl.when(has[d])
        def _():
            pl.semaphore_signal(barrier, inc=1, device_id=dev[d], device_id_type=MESH)

    for k in (2, 3):
        pl.semaphore_signal(barrier, inc=1, device_id=partner[k], device_id_type=MESH)

    def copy(source, target, slot, device):
        return pltpu.make_async_remote_copy(
            src_ref=source, dst_ref=target, send_sem=ssem.at[slot], recv_sem=rsem.at[slot],
            device_id=device, device_id_type=MESH)

    sent = []

    def start(d, source, target, slot):
        @pl.when(has[d])
        def _():
            copy(source, target, slot, dev[d]).start()

        sent.append((d, source, target, slot))

    def arrive(d, source, target, slot):
        @pl.when(has[OPP[d]])
        def _():
            copy(source, target, slot, dev[d]).wait_recv()

    for d in range(4):
        @pl.when(jnp.logical_not(has[OPP[d]]))
        def _():
            crecv[d] = jnp.ones((rows, cols), F32)
            arecv[d] = jnp.zeros((rows, cols), jnp.int32)
            for e in range(NU):
                if d < 2:
                    rowbuf[e, d] = jnp.zeros((members, cols), F32)
                else:
                    colbuf[e, d - 2] = jnp.zeros((rows, cols), F32)
            for e in range(NX0):
                xrecv[e, d] = jnp.zeros((members, cols), F32)

    lane = lax.broadcasted_iota(jnp.int32, (rows, cols), 1)
    sub = lax.broadcasted_iota(jnp.int32, (rows, cols), 0)
    pair_lane = lane // 2

    def u_sources(e):
        return (rsend.at[e, 0], rsend.at[e, 1], csend.at[e], csend.at[e])

    def u_targets(e):
        return (rowbuf.at[e, 0], rowbuf.at[e, 1], colbuf.at[e, 0], colbuf.at[e, 1])

    def pack(e, field_of):
        packed = jnp.zeros((rows, cols), F32)
        for m in range(members):
            v = field_of(m)
            packed = jnp.where(pair_lane == m, pltpu.roll(v, 2 * m + 1, 1), packed)
            rsend[e, 0, m : m + 1, :] = v[0:1]
            rsend[e, 1, m : m + 1, :] = v[rows - 1 : rows]
        csend[e] = packed

    def u_start(e):
        for d in (2, 3, 0, 1):
            start(d, u_sources(e)[d], u_targets(e)[d], 8 + 4 * e + d)

    def u_arrive(e):
        for d in range(4):
            arrive(d, u_sources(e)[d], u_targets(e)[d], 8 + 4 * e + d)

    pack(0, lambda m: guess[m])
    pl.semaphore_wait(barrier, count)
    for d in range(4):
        start(d, cond, crecv.at[d], d)
        start(d, agg, arecv.at[d], 4 + d)
    u_start(0)

    agg_v = agg[...]
    sub64 = lax.broadcasted_iota(jnp.int32, (NA, cols), 0)
    for r in range(rows):
        mo[:, r * cols : (r + 1) * cols] = jnp.where(
            sub64 == agg_v[r : r + 1], 1.0, 0.0).astype(BF16)
    wmat[...] = jnp.zeros(wmat.shape, BF16)
    msend[...] = jnp.zeros(msend.shape, F32)
    xt[...] = jnp.zeros(xt.shape, F32)
    iota128 = lax.broadcasted_iota(jnp.int32, (cols, cols), 0)
    for k in range(LEVELS):
        pmk = pm[k : k + 1, :]
        pmk = jnp.where(upper[k] == 1, pltpu.roll(pmk, NA, 1), pmk)
        qts[k] = jnp.where(iota128 == pmk, 1.0, 0.0).astype(BF16)

    for d in range(4):
        arrive(d, cond, crecv.at[d], d)
        arrive(d, agg, arecv.at[d], 4 + d)
    c = cond[...]

    def face(other):
        return 2.0 * (c * other) / (c + other)

    last = rows - 1
    east = face(jnp.where(lane == cols - 1, pltpu.roll(crecv[2], cols - 1, 1), pltpu.roll(c, cols - 1, 1)))
    west = face(jnp.where(lane == 0, pltpu.roll(crecv[3], 1, 1), pltpu.roll(c, 1, 1)))
    south = face(jnp.where(sub == last, pltpu.roll(crecv[0], last, 0), pltpu.roll(c, last, 0)))
    north = face(jnp.where(sub == 0, pltpu.roll(crecv[1], 1, 0), pltpu.roll(c, 1, 0)))
    hasi = [h.astype(jnp.int32) for h in has]
    north = jnp.where(sub >= 1 - hasi[0], north, 0.0)
    south = jnp.where(sub < last + hasi[1], south, 0.0)
    west = jnp.where(lane >= 1 - hasi[2], west, 0.0)
    east = jnp.where(lane < cols - 1 + hasi[3], east, 0.0)
    diag = sto[...] + east + west + south + north
    step = OMEGA_FINE / diag

    def apply_field(e, finish):
        h_in = jnp.where(lane % 2 == 0, colbuf[e, 1], pltpu.roll(colbuf[e, 0], cols - 2, 1))
        for m in range(members):
            v = u[m]
            hm = pltpu.roll(h_in, (cols - 2 * m) % cols, 1)
            from_w = jnp.where(lane == 0, hm, pltpu.roll(v, 1, 1))
            from_e = jnp.where(lane == cols - 1, hm, pltpu.roll(v, cols - 1, 1))
            from_s = jnp.where(sub == last, rowbuf[e, 0, m : m + 1, :], pltpu.roll(v, last, 0))
            from_n = jnp.where(sub == 0, rowbuf[e, 1, m : m + 1, :], pltpu.roll(v, 1, 0))
            rest = src[m] - (diag * v - (east * from_e + west * from_w + south * from_s + north * from_n))
            finish(m, v, rest)

    def sweep(e):
        def finish(m, v, rest):
            u[m] = v + step * rest

        apply_field(e, finish)
        pack(e + 1, lambda m: u[m])
        u_start(e + 1)

    in_east = jnp.where(lane < cols - 1, east, 0.0)
    in_south = jnp.where(sub < last, south, 0.0)
    right = pltpu.roll(agg_v, cols - 1, 1)
    below = pltpu.roll(agg_v, last, 0)
    half = 0.5 * diag
    for r in range(rows):
        s = slice(r, r + 1)
        g = (jnp.where(sub64 == right[s], in_east[s], 0.0)
             + jnp.where(sub64 == below[s], in_south[s], 0.0)
             - jnp.where(sub64 == agg_v[s], half[s], 0.0))
        for i, part in enumerate(split3(g)):
            gmat[i * NA : (i + 1) * NA, r * cols : (r + 1) * cols] = part
    gx = dg(gmat[...], mo[...], NT)
    xt[0:NA, 0:NA] = gx[0:NA] + (gx[NA : 2 * NA] + gx[2 * NA : 3 * NA])
    xfull = xt[...]
    block = -(xfull + xfull.T)[0:NA]
    msend[0] = block

    def mat_copy(k):
        return copy(msend.at[k], mrecv.at[k], 8 + 4 * (NU + NX0) + k, partner[k])

    def vec_copy(k):
        return copy(vsend.at[k], vrecv.at[k], 8 + 4 * (NU + NX0) + LEVELS + k, partner[k])

    mat_copy(0).start()

    lane_c = lax.broadcasted_iota(jnp.int32, (NA, cols), 1)
    lane_1 = lax.broadcasted_iota(jnp.int32, (1, cols), 1)

    def weight(mat):
        d = jnp.sum(jnp.where(lane_c == sub64, mat, 0.0), axis=0, keepdims=True)
        ok = lane_1 < NA
        return jnp.where(ok, OMEGA_COARSE / jnp.where(ok, d, 1.0), 0.0)

    weights = [weight(block)]

    def next_mat(k):
        mat_copy(k).wait_recv()
        both = jnp.concatenate([msend[k], pltpu.roll(mrecv[k], NA, 1)], axis=0)
        qt = qts[k]
        mat = hot_dot(qt[0:NA], dot_hot(both, qt, NT), NN)
        msend[k + 1] = mat
        if k + 1 < LEVELS:
            mat_copy(k + 1).start()
            hi, lo = split2(mat)
            bsp[k, 0] = hi
            bsp[k, 1] = lo
            weights.append(weight(mat))

    u[...] = guess[...]
    u_arrive(0)
    sweep(0)

    agg_t = agg_v.astype(F32).T.astype(jnp.int32)

    def couple(slot, own_ids, other_ids, faces, width):
        own = jnp.where(lax.broadcasted_iota(jnp.int32, (cols, width), 0) == own_ids, 1.0, 0.0).astype(BF16)
        other = jnp.where(lax.broadcasted_iota(jnp.int32, (NA, width), 0) == other_ids, faces, 0.0)
        hi, lo = split2(-dot_hot(other, own, NT))
        wmat[0, slot * cols : slot * cols + NA] = hi
        wmat[1, slot * cols : slot * cols + NA] = lo

    hi, lo = split2(block)
    wmat[0, 0:NA] = hi
    wmat[1, 0:NA] = lo
    couple(1, agg_v[last : rows], arecv[0][0:1], south[last : rows], cols)
    couple(2, agg_v[0:1], arecv[1][last : rows], north[0:1], cols)
    agg_e = arecv[2].astype(F32).T.astype(jnp.int32)
    agg_w = arecv[3].astype(F32).T.astype(jnp.int32)
    couple(3, agg_t[cols - 1 : cols], agg_e[0:1], east.T[cols - 1 : cols], rows)
    couple(4, agg_t[0:1], agg_w[cols - 1 : cols], west.T[0:1], rows)
    next_mat(0)
    u_arrive(1)
    sweep(1)
    next_mat(1)
    u_arrive(2)
    sweep(2)
    next_mat(2)
    u_arrive(3)

    def keep_left(m, v, rest):
        left[m] = rest

    apply_field(3, keep_left)
    for r in range(rows):
        for i, part in enumerate(split3(left[:, r, :])):
            rlhs[i * members : (i + 1) * members, r * cols : (r + 1) * cols] = part
    gr = dg(rlhs[...], mo[...], NT)
    vsend[LEVELS] = jnp.zeros((members, cols), F32)
    vsend[LEVELS, :, 0:NA] = gr[0:members] + (gr[members : 2 * members] + gr[2 * members : 3 * members])
    y0 = vsend[LEVELS]

    def x_slot(e, d):
        return (d, xsend.at[e], xrecv.at[e, d], 8 + 4 * NU + 4 * e + d)

    def level_one(e, x, between=None):
        xsend[e] = x
        for d in (2, 3, 0, 1):
            start(*x_slot(e, d))
        if between is not None:
            between()
        for d in range(4):
            arrive(*x_slot(e, d))
        every = jnp.concatenate([x] + [xrecv[e, d] for d in range(4)], axis=1)
        return dot_parts(every, wmat[0], wmat[1])

    inverse = []

    def last_mat():
        next_mat(3)
        mat = jnp.where(lane_c < NA, msend[LEVELS], jnp.where(lane_c - NA == sub64, 1.0, 0.0))
        for k in range(NA):
            pivot = mat[k : k + 1] / mat[k : k + 1, k : k + 1]
            mat = jnp.where(sub64 == k, pivot, mat - mat[:, k : k + 1] * pivot)
        inverse.append(jnp.where(lane_c < NA, pltpu.roll(mat, NA, 1), 0.0))

    x = y0 * weights[0]
    x = x + (y0 - level_one(0, x, last_mat)) * weights[0]
    x = x + (y0 - level_one(1, x)) * weights[0]
    rem = y0 - level_one(2, x)
    sols, rhss = [x], [y0]
    for k in range(LEVELS):
        vsend[k] = rem
        vec_copy(k).start()
        vec_copy(k).wait_recv()
        y = dot_hot(rem + pltpu.roll(vrecv[k], NA, 1), qts[k], NT)
        rhss.append(y)
        if k < LEVELS - 1:
            apply_c = lambda z: dot_parts(z[:, 0:NA], bsp[k, 0], bsp[k, 1])
            w = weights[k + 1]
            x = y * w
            for _ in range(SWEEPS - 1):
                x = x + (y - apply_c(x)) * w
            rem = y - apply_c(x)
        else:
            x = lax.dot_general(y[:, 0:NA], inverse[0], NN, precision=lax.Precision.HIGHEST,
                                preferred_element_type=F32)
        sols.append(x)
    lane_m = lax.broadcasted_iota(jnp.int32, (members, cols), 1)
    for k in reversed(range(LEVELS)):
        x = sols[k] + jnp.where(lane_m < NA, dot_hot(x, qts[k], NN), 0.0)
        for i in range(SWEEPS):
            if k > 0:
                applied = dot_parts(x[:, 0:NA], bsp[k - 1, 0], bsp[k - 1, 1])
            else:
                applied = level_one(SWEEPS + i, x)
            x = x + (rhss[k] - applied) * weights[k]

    for r in range(rows):
        part = dot_hot(x[:, 0:NA], mo[:, r * cols : (r + 1) * cols], NN)
        u[:, r, :] = u[:, r, :] + part
    first = SWEEPS + 1
    pack(first, lambda m: u[m])
    u_start(first)
    for i in range(SWEEPS):
        u_arrive(first + i)
        sweep(first + i)
    u_arrive(first + SWEEPS)

    def out(m, v, rest):
        sol[m] = v
        res[m] = rest

    apply_field(first + SWEEPS, out)
    for d, source, target, slot in sent:
        @pl.when(has[d])
        def _():
            copy(source, target, slot, dev[d]).wait_send()

    for k in range(LEVELS):
        mat_copy(k).wait_send()
        vec_copy(k).wait_send()


def shards(n_row, n_col, source, guess, conductivity, storage, aggregates, pair_maps):
    members, rows, cols = source.shape
    cells = rows * cols
    vm = pl.BlockSpec(memory_space=pltpu.VMEM)
    slots = 8 + 4 * (NU + NX0) + 2 * LEVELS
    return pl.pallas_call(
        functools.partial(kernel, n_row, n_col),
        out_shape=(jax.ShapeDtypeStruct(source.shape, F32),) * 2,
        in_specs=[vm] * 6,
        out_specs=(vm, vm),
        scratch_shapes=[
            pltpu.VMEM((members, rows, cols), F32),
            pltpu.VMEM((members, rows, cols), F32),
            pltpu.VMEM((NA, cells), BF16),
            pltpu.VMEM((3 * NA, cells), BF16),
            pltpu.VMEM((3 * members, cells), BF16),
            pltpu.VMEM((cols, cols), F32),
            pltpu.VMEM((4, rows, cols), F32),
            pltpu.VMEM((4, rows, cols), jnp.int32),
            pltpu.VMEM((NU, 2, members, cols), F32),
            pltpu.VMEM((NU, 2, rows, cols), F32),
            pltpu.VMEM((NU, 2, members, cols), F32),
            pltpu.VMEM((NU, rows, cols), F32),
            pltpu.VMEM((NX0, members, cols), F32),
            pltpu.VMEM((NX0, 4, members, cols), F32),
            pltpu.VMEM((LEVELS + 1, NA, cols), F32),
            pltpu.VMEM((LEVELS, NA, cols), F32),
            pltpu.VMEM((LEVELS + 1, members, cols), F32),
            pltpu.VMEM((LEVELS, members, cols), F32),
            pltpu.VMEM((2, 5 * cols, cols), BF16),
            pltpu.VMEM((LEVELS - 1, 2, NA, cols), BF16),
            pltpu.VMEM((LEVELS, cols, cols), BF16),
            pltpu.SemaphoreType.DMA((slots,)),
            pltpu.SemaphoreType.DMA((slots,)),
        ],
        compiler_params=pltpu.CompilerParams(collective_id=0, has_side_effects=True),
    )(source, guess, conductivity, storage, aggregates, pair_maps.reshape(LEVELS, -1))


def solution(mesh):
    placed = (
        P(None, "row", "col"),
        P(None, "row", "col"),
        P("row", "col"),
        P("row", "col"),
        P("row", "col"),
        P(None, "row", "col", None),
    )
    return jax.shard_map(
        functools.partial(shards, mesh.shape["row"], mesh.shape["col"]),
        mesh=mesh,
        in_specs=placed,
        out_specs=(P(None, "row", "col"), P(None, "row", "col")),
        check_vma=False,
    )
```

time: 392 us -> 77.9 us (0.20)
  waiting for transfers between devices: 209 us -> 0 us
  starting transfers between devices: 132 us -> 0 us
  Pallas kernels: 0 us -> 74.6 us
  other arithmetic: 19 us -> 0 us
  matrix products: 18.5 us -> 0 us
  local copies, waits for them, and re-layouts: 10 us -> 2.42 us
    ppermute x68 -> x0, waiting for transfers between devices: 209 us -> none  [the longest x30 138 us: with_halo(): lax.ppermute(head, axis, [((i + 1) % count, i) for i in range(ends)])]
    ppermute x68 -> x0, starting transfers between devices: 132 us -> none  [the longest x30 82.6 us: with_halo(): lax.ppermute(tail, axis, [(i, (i + 1) % count) for i in range(ends)])]
    pallas_call x0 -> x1, Pallas kernels: none -> 74.6 us  [shards(): pl.pallas_call(functools.partial(kernel, n_row, n_col), out_shape=(jax.Sh...]
    dot_general x63 -> x0, matrix products: 18 us -> none  [the longest x9 6.41 us: pair_sum(): lax.dot_general(left, right, (((1,), (1,)), ((), ())), precision=HIGHEST)]
    another operation x5 -> x0, other arithmetic: 12.1 us -> none  [the longest x3 6.51 us: shards(): factor = jnp.linalg.cholesky(coarse_mat)]
    slice x34 -> x0, local copies, waits for them, and re-layouts: 4.01 us -> none  [the longest x28 3.29 us: with_halo(): head = lax.slice_in_dim(cells, 0, width, axis=dim)]
  transfers between devices with their start and end apart: 68 -> 0, of which waited for: 44 -> 0; matrix products, arithmetic and copies ran while one was open for 6% -> 0% of each run, Pallas kernels for 0% -> 0%
where the time goes in v1:
time: 77.9 us; the launch traced here: 77.7 us
  Pallas kernels  74.6 us (96%)
  local copies, waits for them, and re-layouts  2.42 us (3%)
    pallas_call x1, Pallas kernels, shards(): pl.pallas_call(functools.partial(kernel, n_row, n_col), out_shape=(jax.Sh...  74.6 us
    unnamed x4, local copies, waits for them, and re-layouts  2.42 us

profile of v1, /device:TPU:0, one launch (start us, length us, event | category | flops | bytes accessed | tf_op | source)
XLA Modules:
  0.0 77.7 jit_solution(7285656193553651378)
XLA Ops:
  0.6 74.6 %shard_map.77 = (f32[16,32,128]{2,1,0:T(8,128)}, f32[16,32,128]{2,1,0:T(8,128)}) custom-call(f32[16,32,128]{2,1,0:T(8,128)} %src.1, f32[16,32,128]{2,1,0:T(8,128)} %guess.1, f32[32,128]{1,0:T(8,128)} %cond.1, f32[32,128]{1,0:T(8,128)} %sto.1, s32[32,128]{1,0:T(8,128)} %agg.1, s32[4,128]{1,0:T(4,128)} %bitcast.1), custom_call_target="tpu_custom_call" | custom-call | tf_op jit(solution)/shard_map/pallas_call | solution.py:388
  75.3 0.0 copy-start
  75.3 1.7 %copy.10 = f32[16,32,128]{2,1,0:T(8,128)} copy(f32[16,32,128]{2,1,0:T(8,128)} %get-tuple-element.4) | data formatting | bytes 524288
  77.0 0.0 copy-done
  77.0 0.7 copy.11
Async XLA Ops:
  75.3 1.7 %copy-start = (f32[16,32,128]{2,1,0:T(8,128)S(1)}, f32[16,32,128]{2,1,0:T(8,128)}, u32[]{:S(2)}) copy-start(f32[16,32,128]{2,1,0:T(8,128)} %get-tuple-element.5) | copy-start | bytes 786436

commit v2 on v1

--- a/solution.py
+++ b/solution.py
@@ -15,8 +15,9 @@
 F32 = jnp.float32
 BF16 = jnp.bfloat16
 MESH = pl.DeviceIdType.MESH
-OPP = (1, 0, 3, 2)
-NU = 2 * (SWEEPS + 1)
+OPP = (1, 0, 3, 2, 7, 6, 5, 4)
+WIDE = SWEEPS + 1
+GROUP = 2 * WIDE
 NX0 = 2 * SWEEPS
 NN = (((1,), (0,)), ((), ()))
 NT = (((1,), (1,)), ((), ()))
@@ -54,13 +55,18 @@
 
 
 def kernel(n_row, n_col, src, guess, cond, sto, agg, pm, sol, res,
-           u, left, mo, gmat, rlhs, xt, crecv, arecv, rowbuf, colbuf, rsend, csend,
-           xsend, xrecv, msend, mrecv, vsend, vrecv, wmat, bsp, qts, ssem, rsem):
+           u, se, left, mo, gmat, rlhs, xt, crecv, srecv, ccorn, scorn, arecv, rowbuf, colbuf, corner,
+           rsend, csend, xsend, xrecv, msend, mrecv, vsend, vrecv, wmat, bsp, qts, ssem, rsem):
     members, rows, cols = guess.shape
+    ext = rows + GROUP
     row = lax.axis_index("row")
     col = lax.axis_index("col")
-    has = (row > 0, row < n_row - 1, col > 0, col < n_col - 1)
-    dev = ((row - 1, col), (row + 1, col), (row, col - 1), (row, col + 1))
+    has = [row > 0, row < n_row - 1, col > 0, col < n_col - 1]
+    dev = [(row - 1, col), (row + 1, col), (row, col - 1), (row, col + 1)]
+    for v in (0, 1):
+        for h in (2, 3):
+            has.append(jnp.logical_and(has[v], has[h]))
+            dev.append((dev[v][0], dev[h][1]))
     col_bit = col % 2
     row_bit = row % 2
     col_bit2 = col // 2 % 2
@@ -75,7 +81,7 @@
 
     barrier = pltpu.get_barrier_semaphore()
     count = jnp.int32(2)
-    for d in range(4):
+    for d in range(8):
         count = count + has[d].astype(jnp.int32)
 
         @pl.when(has[d])
@@ -104,52 +110,107 @@
         def _():
             copy(source, target, slot, dev[d]).wait_recv()
 
-    for d in range(4):
+    for d in range(8):
         @pl.when(jnp.logical_not(has[OPP[d]]))
         def _():
-            crecv[d] = jnp.ones((rows, cols), F32)
-            arecv[d] = jnp.zeros((rows, cols), jnp.int32)
-            for e in range(NU):
+            for got, got_corner in ((crecv, ccorn), (srecv, scorn)):
+                if d < 4:
+                    got[d] = jnp.ones((rows, cols), F32)
+                else:
+                    got_corner[d - 4] = jnp.ones((GROUP, cols), F32)
+            if d < 4:
+                arecv[d] = jnp.zeros((rows, cols), jnp.int32)
+                for e in range(NX0):
+                    xrecv[e, d] = jnp.zeros((members, cols), F32)
+            for p in range(3):
                 if d < 2:
-                    rowbuf[e, d] = jnp.zeros((members, cols), F32)
+                    rowbuf[p, d] = jnp.zeros((WIDE * members, cols), F32)
+                elif d < 4:
+                    colbuf[p, d - 2] = jnp.zeros((rows, cols), F32)
                 else:
-                    colbuf[e, d - 2] = jnp.zeros((rows, cols), F32)
-            for e in range(NX0):
-                xrecv[e, d] = jnp.zeros((members, cols), F32)
-
-    lane = lax.broadcasted_iota(jnp.int32, (rows, cols), 1)
-    sub = lax.broadcasted_iota(jnp.int32, (rows, cols), 0)
-    pair_lane = lane // 2
-
-    def u_sources(e):
-        return (rsend.at[e, 0], rsend.at[e, 1], csend.at[e], csend.at[e])
-
-    def u_targets(e):
-        return (rowbuf.at[e, 0], rowbuf.at[e, 1], colbuf.at[e, 0], colbuf.at[e, 1])
-
-    def pack(e, field_of):
+                    corner[p, d - 4] = jnp.zeros((GROUP, cols), F32)
+
+    lane = lax.broadcasted_iota(jnp.int32, (ext, cols), 1)
+    sub = lax.broadcasted_iota(jnp.int32, (ext, cols), 0)
+    l8 = lane % GROUP
+    owner = lane // GROUP
+    lane8 = lane[0:GROUP]
+    sub8 = sub[0:GROUP]
+
+    def mirror(x):
+        where = lax.broadcasted_iota(jnp.int32, x.shape, 1)
+        bit = 1
+        while bit < GROUP:
+            x = jnp.where(where // bit % 2 == 0, pltpu.roll(x, cols - bit, 1), pltpu.roll(x, bit, 1))
+            bit *= 2
+        return x
+
+    def repeat(x):
+        width = GROUP
+        while width < cols:
+            x = x + pltpu.roll(x, width, 1)
+            width *= 2
+        return x
+
+    def halo_ref(p, d):
+        source = rsend.at[p, d] if d < 2 else csend.at[p] if d < 4 else csend.at[
+            p, pl.ds(0 if d < 6 else rows - GROUP, GROUP)]
+        target = rowbuf.at[p, d] if d < 2 else colbuf.at[p, d - 2] if d < 4 else corner.at[p, d - 4]
+        return d, source, target, 20 + 8 * p + d
+
+    def part_ref(value, plane, corners, d, slot):
+        if d in (2, 3):
+            return d, value, plane.at[d], slot
+        source = value.at[pl.ds(0 if d in (0, 4, 5) else rows - GROUP, GROUP)]
+        target = plane.at[d, pl.ds(0, GROUP)] if d < 2 else corners.at[d - 4]
+        return d, source, target, slot
+
+    def pack(p, field_of):
         packed = jnp.zeros((rows, cols), F32)
         for m in range(members):
             v = field_of(m)
-            packed = jnp.where(pair_lane == m, pltpu.roll(v, 2 * m + 1, 1), packed)
-            rsend[e, 0, m : m + 1, :] = v[0:1]
-            rsend[e, 1, m : m + 1, :] = v[rows - 1 : rows]
-        csend[e] = packed
-
-    def u_start(e):
-        for d in (2, 3, 0, 1):
-            start(d, u_sources(e)[d], u_targets(e)[d], 8 + 4 * e + d)
-
-    def u_arrive(e):
-        for d in range(4):
-            arrive(d, u_sources(e)[d], u_targets(e)[d], 8 + 4 * e + d)
+            packed = jnp.where(owner[0:rows] == m, pltpu.roll(v, (GROUP * m + WIDE) % cols, 1), packed)
+            rsend[p, 0, WIDE * m : WIDE * (m + 1), :] = v[0:WIDE]
+            rsend[p, 1, WIDE * m : WIDE * (m + 1), :] = v[rows - WIDE : rows]
+        csend[p] = mirror(packed)
+
+    order = (2, 3, 4, 5, 6, 7, 0, 1)
+
+    def halo_start(p):
+        for d in order:
+            start(*halo_ref(p, d))
+
+    def halo_arrive(p):
+        for d in range(8):
+            arrive(*halo_ref(p, d))
+
+    def under(south, north):
+        return jnp.where(sub8 < WIDE, south, north)
+
+    def halo_fill(p, field):
+        for m in range(members):
+            field[m, rows : rows + WIDE, :] = rowbuf[p, 0, WIDE * m : WIDE * (m + 1), :]
+            field[m, rows + WIDE : ext, :] = rowbuf[p, 1, WIDE * m : WIDE * (m + 1), :]
+        side_e = jnp.concatenate([colbuf[p, 0], under(corner[p, 0], corner[p, 2])], axis=0)
+        side_w = jnp.concatenate([colbuf[p, 1], under(corner[p, 1], corner[p, 3])], axis=0)
+        return jnp.where(l8 < WIDE, side_e, side_w)
+
+    def cond_parts(d):
+        return part_ref(cond, crecv, ccorn, d, d)
+
+    def sto_parts(d):
+        return part_ref(sto, srecv, scorn, d, 8 + d)
 
     pack(0, lambda m: guess[m])
     pl.semaphore_wait(barrier, count)
+    for d in order:
+        start(*cond_parts(d))
+        start(*sto_parts(d))
+    halo_start(0)
     for d in range(4):
-        start(d, cond, crecv.at[d], d)
-        start(d, agg, arecv.at[d], 4 + d)
-    u_start(0)
+        start(d, agg, arecv.at[d], 16 + d)
+    pack(1, lambda m: src[m])
+    halo_start(1)
 
     agg_v = agg[...]
     sub64 = lax.broadcasted_iota(jnp.int32, (NA, cols), 0)
@@ -165,46 +226,77 @@
         pmk = jnp.where(upper[k] == 1, pltpu.roll(pmk, NA, 1), pmk)
         qts[k] = jnp.where(iota128 == pmk, 1.0, 0.0).astype(BF16)
 
-    for d in range(4):
-        arrive(d, cond, crecv.at[d], d)
-        arrive(d, agg, arecv.at[d], 4 + d)
-    c = cond[...]
-
-    def face(other):
-        return 2.0 * (c * other) / (c + other)
-
+    for d in range(8):
+        arrive(*cond_parts(d))
+        arrive(*sto_parts(d))
+
+    def extend(value, plane, corners):
+        main = jnp.concatenate([value[...], under(plane[0, 0:GROUP], plane[1, 0:GROUP])], axis=0)
+        side_e = jnp.concatenate([plane[2], under(corners[0], corners[2])], axis=0)
+        side_w = jnp.concatenate([plane[3], under(corners[1], corners[3])], axis=0)
+        base = jnp.where(lane < WIDE, pltpu.roll(side_w, WIDE, 1), pltpu.roll(side_e, WIDE, 1))
+        side = mirror(repeat(jnp.where(lane < GROUP, base, 0.0)))
+        return main, side
+
+    cm, cs = extend(cond, crecv, ccorn)
+    sm, ss = extend(sto, srecv, scorn)
     last = rows - 1
-    east = face(jnp.where(lane == cols - 1, pltpu.roll(crecv[2], cols - 1, 1), pltpu.roll(c, cols - 1, 1)))
-    west = face(jnp.where(lane == 0, pltpu.roll(crecv[3], 1, 1), pltpu.roll(c, 1, 1)))
-    south = face(jnp.where(sub == last, pltpu.roll(crecv[0], last, 0), pltpu.roll(c, last, 0)))
-    north = face(jnp.where(sub == 0, pltpu.roll(crecv[1], 1, 0), pltpu.roll(c, 1, 0)))
-    hasi = [h.astype(jnp.int32) for h in has]
-    north = jnp.where(sub >= 1 - hasi[0], north, 0.0)
-    south = jnp.where(sub < last + hasi[1], south, 0.0)
+    hasi = [h.astype(jnp.int32) for h in has[0:4]]
+
+    def face(a, b):
+        return 2.0 * (a * b) / (a + b)
+
+    def vertical(x):
+        down = jnp.where(jnp.logical_and(sub == last, hasi[1] == 0), 0.0, face(x, pltpu.roll(x, ext - 1, 0)))
+        up = jnp.where(jnp.logical_and(sub == 0, hasi[0] == 0), 0.0, face(x, pltpu.roll(x, 1, 0)))
+        return down, up
+
+    side_at = pltpu.roll(cs, cols - WIDE, 1)
+    rim = jnp.logical_and(lane >= WIDE - 1, lane <= WIDE)
+    main_at = repeat(jnp.where(rim, pltpu.roll(cm, WIDE, 1), 0.0))
+    east = face(cm, jnp.where(lane == cols - 1, side_at, pltpu.roll(cm, cols - 1, 1)))
+    west = face(cm, jnp.where(lane == 0, side_at, pltpu.roll(cm, 1, 1)))
+    east = jnp.where(lane < cols - 1 + hasi[3], east, 0.0)
     west = jnp.where(lane >= 1 - hasi[2], west, 0.0)
-    east = jnp.where(lane < cols - 1 + hasi[3], east, 0.0)
-    diag = sto[...] + east + west + south + north
+    south, north = vertical(cm)
+    diag = sm + east + west + south + north
     step = OMEGA_FINE / diag
-
-    def apply_field(e, finish):
-        h_in = jnp.where(lane % 2 == 0, colbuf[e, 1], pltpu.roll(colbuf[e, 0], cols - 2, 1))
+    s_west = face(cs, jnp.where(l8 == WIDE - 1, main_at, pltpu.roll(cs, cols - 1, 1)))
+    s_east = face(cs, jnp.where(l8 == WIDE, main_at, pltpu.roll(cs, 1, 1)))
+    s_west = jnp.where(jnp.logical_and(l8 == WIDE - 1, hasi[3] == 0), 0.0, s_west)
+    s_east = jnp.where(jnp.logical_and(l8 == WIDE, hasi[2] == 0), 0.0, s_east)
+    s_south, s_north = vertical(cs)
+    s_diag = ss + s_east + s_west + s_south + s_north
+    s_step = OMEGA_FINE / s_diag
+
+    def apply_field(side, n, finish):
+        lane_n = lane[0:n]
+        edge = jnp.zeros((ext, cols), F32)
         for m in range(members):
             v = u[m]
-            hm = pltpu.roll(h_in, (cols - 2 * m) % cols, 1)
-            from_w = jnp.where(lane == 0, hm, pltpu.roll(v, 1, 1))
-            from_e = jnp.where(lane == cols - 1, hm, pltpu.roll(v, cols - 1, 1))
-            from_s = jnp.where(sub == last, rowbuf[e, 0, m : m + 1, :], pltpu.roll(v, last, 0))
-            from_n = jnp.where(sub == 0, rowbuf[e, 1, m : m + 1, :], pltpu.roll(v, 1, 0))
-            rest = src[m] - (diag * v - (east * from_e + west * from_w + south * from_s + north * from_n))
-            finish(m, v, rest)
-
-    def sweep(e):
+            hm = pltpu.roll(side, (2 * cols - GROUP * m - WIDE) % cols, 1)[0:n]
+            vn = v[0:n]
+            from_w = jnp.where(lane_n == 0, hm, pltpu.roll(vn, 1, 1))
+            from_e = jnp.where(lane_n == cols - 1, hm, pltpu.roll(vn, cols - 1, 1))
+            from_s = pltpu.roll(v, ext - 1, 0)[0:n]
+            from_n = pltpu.roll(v, 1, 0)[0:n]
+            rest = se[m, 0:n] - (diag[0:n] * vn - (
+                east[0:n] * from_e + west[0:n] * from_w + south[0:n] * from_s + north[0:n] * from_n))
+            if n == ext:
+                edge = jnp.where(owner == m, pltpu.roll(v, (GROUP * m + WIDE) % cols, 1), edge)
+            finish(m, vn, rest)
+        return edge
+
+    def sweep(side, s_src):
         def finish(m, v, rest):
             u[m] = v + step * rest
 
-        apply_field(e, finish)
-        pack(e + 1, lambda m: u[m])
-        u_start(e + 1)
+        edge = apply_field(side, ext, finish)
+        from_w = jnp.where(l8 == WIDE - 1, edge, pltpu.roll(side, cols - 1, 1))
+        from_e = jnp.where(l8 == WIDE, edge, pltpu.roll(side, 1, 1))
+        rest = s_src - (s_diag * side - (s_east * from_e + s_west * from_w
+                        + s_south * pltpu.roll(side, ext - 1, 0) + s_north * pltpu.roll(side, 1, 0)))
+        return side + s_step * rest
 
     in_east = jnp.where(lane < cols - 1, east, 0.0)
     in_south = jnp.where(sub < last, south, 0.0)
@@ -225,10 +317,10 @@
     msend[0] = block
 
     def mat_copy(k):
-        return copy(msend.at[k], mrecv.at[k], 8 + 4 * (NU + NX0) + k, partner[k])
+        return copy(msend.at[k], mrecv.at[k], 44 + 4 * NX0 + k, partner[k])
 
     def vec_copy(k):
-        return copy(vsend.at[k], vrecv.at[k], 8 + 4 * (NU + NX0) + LEVELS + k, partner[k])
+        return copy(vsend.at[k], vrecv.at[k], 44 + 4 * NX0 + LEVELS + k, partner[k])
 
     mat_copy(0).start()
 
@@ -255,10 +347,8 @@
             bsp[k, 1] = lo
             weights.append(weight(mat))
 
-    u[...] = guess[...]
-    u_arrive(0)
-    sweep(0)
-
+    for d in range(4):
+        arrive(d, agg, arecv.at[d], 16 + d)
     agg_t = agg_v.astype(F32).T.astype(jnp.int32)
 
     def couple(slot, own_ids, other_ids, faces, width):
@@ -271,25 +361,26 @@
     hi, lo = split2(block)
     wmat[0, 0:NA] = hi
     wmat[1, 0:NA] = lo
-    couple(1, agg_v[last : rows], arecv[0][0:1], south[last : rows], cols)
+    couple(1, agg_v[last:rows], arecv[0][0:1], south[last:rows], cols)
     couple(2, agg_v[0:1], arecv[1][last : rows], north[0:1], cols)
     agg_e = arecv[2].astype(F32).T.astype(jnp.int32)
     agg_w = arecv[3].astype(F32).T.astype(jnp.int32)
-    couple(3, agg_t[cols - 1 : cols], agg_e[0:1], east.T[cols - 1 : cols], rows)
-    couple(4, agg_t[0:1], agg_w[cols - 1 : cols], west.T[0:1], rows)
-    next_mat(0)
-    u_arrive(1)
-    sweep(1)
-    next_mat(1)
-    u_arrive(2)
-    sweep(2)
-    next_mat(2)
-    u_arrive(3)
+    couple(3, agg_t[cols - 1 : cols], agg_e[0:1], east[0:rows].T[cols - 1 : cols], rows)
+    couple(4, agg_t[0:1], agg_w[cols - 1 : cols], west[0:rows].T[0:1], rows)
+    for m in range(members):
+        u[m, 0:rows] = guess[m]
+        se[m, 0:rows] = src[m]
+    halo_arrive(0)
+    side = halo_fill(0, u)
+    halo_arrive(1)
+    s_src = halo_fill(1, se)
+    for _ in range(SWEEPS):
+        side = sweep(side, s_src)
 
     def keep_left(m, v, rest):
         left[m] = rest
 
-    apply_field(3, keep_left)
+    apply_field(side, rows, keep_left)
     for r in range(rows):
         for i, part in enumerate(split3(left[:, r, :])):
             rlhs[i * members : (i + 1) * members, r * cols : (r + 1) * cols] = part
@@ -299,7 +390,7 @@
     y0 = vsend[LEVELS]
 
     def x_slot(e, d):
-        return (d, xsend.at[e], xrecv.at[e, d], 8 + 4 * NU + 4 * e + d)
+        return (d, xsend.at[e], xrecv.at[e, d], 44 + 4 * e + d)
 
     def level_one(e, x, between=None):
         xsend[e] = x
@@ -323,13 +414,15 @@
         inverse.append(jnp.where(lane_c < NA, pltpu.roll(mat, NA, 1), 0.0))
 
     x = y0 * weights[0]
-    x = x + (y0 - level_one(0, x, last_mat)) * weights[0]
-    x = x + (y0 - level_one(1, x)) * weights[0]
-    rem = y0 - level_one(2, x)
+    x = x + (y0 - level_one(0, x, lambda: next_mat(0))) * weights[0]
+    x = x + (y0 - level_one(1, x, lambda: next_mat(1))) * weights[0]
+    rem = y0 - level_one(2, x, lambda: next_mat(2))
     sols, rhss = [x], [y0]
     for k in range(LEVELS):
         vsend[k] = rem
         vec_copy(k).start()
+        if k == 1:
+            last_mat()
         vec_copy(k).wait_recv()
         y = dot_hot(rem + pltpu.roll(vrecv[k], NA, 1), qts[k], NT)
         rhss.append(y)
@@ -357,19 +450,18 @@
     for r in range(rows):
         part = dot_hot(x[:, 0:NA], mo[:, r * cols : (r + 1) * cols], NN)
         u[:, r, :] = u[:, r, :] + part
-    first = SWEEPS + 1
-    pack(first, lambda m: u[m])
-    u_start(first)
-    for i in range(SWEEPS):
-        u_arrive(first + i)
-        sweep(first + i)
-    u_arrive(first + SWEEPS)
+    pack(2, lambda m: u[m, 0:rows])
+    halo_start(2)
+    halo_arrive(2)
+    side = halo_fill(2, u)
+    for _ in range(SWEEPS):
+        side = sweep(side, s_src)
 
     def out(m, v, rest):
         sol[m] = v
         res[m] = rest
 
-    apply_field(first + SWEEPS, out)
+    apply_field(side, rows, out)
     for d, source, target, slot in sent:
         @pl.when(has[d])
         def _():
@@ -383,26 +475,32 @@
 def shards(n_row, n_col, source, guess, conductivity, storage, aggregates, pair_maps):
     members, rows, cols = source.shape
     cells = rows * cols
+    ext = rows + GROUP
     vm = pl.BlockSpec(memory_space=pltpu.VMEM)
-    slots = 8 + 4 * (NU + NX0) + 2 * LEVELS
+    slots = 44 + 4 * NX0 + 2 * LEVELS
     return pl.pallas_call(
         functools.partial(kernel, n_row, n_col),
         out_shape=(jax.ShapeDtypeStruct(source.shape, F32),) * 2,
         in_specs=[vm] * 6,
         out_specs=(vm, vm),
         scratch_shapes=[
-            pltpu.VMEM((members, rows, cols), F32),
+            pltpu.VMEM((members, ext, cols), F32),
+            pltpu.VMEM((members, ext, cols), F32),
             pltpu.VMEM((members, rows, cols), F32),
             pltpu.VMEM((NA, cells), BF16),
             pltpu.VMEM((3 * NA, cells), BF16),
             pltpu.VMEM((3 * members, cells), BF16),
             pltpu.VMEM((cols, cols), F32),
             pltpu.VMEM((4, rows, cols), F32),
+            pltpu.VMEM((4, rows, cols), F32),
+            pltpu.VMEM((4, GROUP, cols), F32),
+            pltpu.VMEM((4, GROUP, cols), F32),
             pltpu.VMEM((4, rows, cols), jnp.int32),
-            pltpu.VMEM((NU, 2, members, cols), F32),
-            pltpu.VMEM((NU, 2, rows, cols), F32),
-            pltpu.VMEM((NU, 2, members, cols), F32),
-            pltpu.VMEM((NU, rows, cols), F32),
+            pltpu.VMEM((3, 2, WIDE * members, cols), F32),
+            pltpu.VMEM((3, 2, rows, cols), F32),
+            pltpu.VMEM((3, 4, GROUP, cols), F32),
+            pltpu.VMEM((3, 2, WIDE * members, cols), F32),
+            pltpu.VMEM((3, rows, cols), F32),
             pltpu.VMEM((NX0, members, cols), F32),
             pltpu.VMEM((NX0, 4, members, cols), F32),
             pltpu.VMEM((LEVELS + 1, NA, cols), F32),

time: 77.9 us -> 65.4 us (0.84)
  Pallas kernels: 74.6 us -> 62.1 us
    pallas_call x1, Pallas kernels: 74.6 us -> 62.1 us  [shards(): pl.pallas_call(functools.partial(kernel, n_row, n_col), out_shape=(jax.Sh...]
where the time goes in v2:
time: 65.4 us; the launch traced here: 65.2 us
  Pallas kernels  62.1 us (95%)
  local copies, waits for them, and re-layouts  2.42 us (4%)
    pallas_call x1, Pallas kernels, shards(): pl.pallas_call(functools.partial(kernel, n_row, n_col), out_shape=(jax.Sh...  62.1 us
    unnamed x4, local copies, waits for them, and re-layouts  2.42 us

profile of v2, /device:TPU:0, one launch (start us, length us, event | category | flops | bytes accessed | tf_op | source)
XLA Modules:
  0.0 65.2 jit_solution(11153385843985358847)
XLA Ops:
  0.6 62.1 %shard_map.77 = (f32[16,32,128]{2,1,0:T(8,128)}, f32[16,32,128]{2,1,0:T(8,128)}) custom-call(f32[16,32,128]{2,1,0:T(8,128)} %src.1, f32[16,32,128]{2,1,0:T(8,128)} %guess.1, f32[32,128]{1,0:T(8,128)} %cond.1, f32[32,128]{1,0:T(8,128)} %sto.1, s32[32,128]{1,0:T(8,128)} %agg.1, s32[4,128]{1,0:T(4,128)} %bitcast.1), custom_call_target="tpu_custom_call" | custom-call | tf_op jit(solution)/shard_map/pallas_call | solution.py:481
  62.8 0.0 copy-start
  62.8 1.7 %copy.10 = f32[16,32,128]{2,1,0:T(8,128)} copy(f32[16,32,128]{2,1,0:T(8,128)} %get-tuple-element.4) | data formatting | bytes 524288
  64.5 0.0 copy-done
  64.5 0.7 %copy.11 = f32[16,32,128]{2,1,0:T(8,128)} copy(f32[16,32,128]{2,1,0:T(8,128)S(1)} %copy-done) | data formatting | bytes 524288
Async XLA Ops:
  62.8 1.7 %copy-start = (f32[16,32,128]{2,1,0:T(8,128)S(1)}, f32[16,32,128]{2,1,0:T(8,128)}, u32[]{:S(2)}) copy-start(f32[16,32,128]{2,1,0:T(8,128)} %get-tuple-element.5) | copy-start | bytes 786436

commit v3 on v2

--- a/solution.py
+++ b/solution.py
@@ -39,9 +39,9 @@
     return hi, mid, (rest - mid.astype(F32)).astype(BF16)
 
 
-def dot_parts(x, w_hi, w_lo):
+def dot_parts(x, w_hi, w_lo, dims=NN):
     hi, lo = split2(x)
-    return dg(hi, w_hi, NN) + (dg(lo, w_hi, NN) + dg(hi, w_lo, NN))
+    return dg(hi, w_hi, dims) + (dg(lo, w_hi, dims) + dg(hi, w_lo, dims))
 
 
 def dot_hot(x, hot, dims):
@@ -202,14 +202,15 @@
         return part_ref(sto, srecv, scorn, d, 8 + d)
 
     pack(0, lambda m: guess[m])
+    pack(1, lambda m: src[m])
     pl.semaphore_wait(barrier, count)
     for d in order:
         start(*cond_parts(d))
+    for d in range(4):
+        start(d, agg, arecv.at[d], 16 + d)
+    for d in order:
         start(*sto_parts(d))
     halo_start(0)
-    for d in range(4):
-        start(d, agg, arecv.at[d], 16 + d)
-    pack(1, lambda m: src[m])
     halo_start(1)
 
     agg_v = agg[...]
@@ -226,6 +227,28 @@
         pmk = jnp.where(upper[k] == 1, pltpu.roll(pmk, NA, 1), pmk)
         qts[k] = jnp.where(iota128 == pmk, 1.0, 0.0).astype(BF16)
 
+    def face(a, b):
+        return 2.0 * (a * b) / (a + b)
+
+    last = rows - 1
+    c = cond[...]
+    in_east = jnp.where(lane[0:rows] < cols - 1, face(c, pltpu.roll(c, cols - 1, 1)), 0.0)
+    in_south = jnp.where(sub[0:rows] < last, face(c, pltpu.roll(c, last, 0)), 0.0)
+    right = pltpu.roll(agg_v, cols - 1, 1)
+    below = pltpu.roll(agg_v, last, 0)
+    half = 0.5 * (sto[...] + in_east + pltpu.roll(in_east, 1, 1) + in_south + pltpu.roll(in_south, 1, 0))
+    for r in range(rows):
+        s = slice(r, r + 1)
+        g = (jnp.where(sub64 == right[s], in_east[s], 0.0)
+             + jnp.where(sub64 == below[s], in_south[s], 0.0)
+             - jnp.where(sub64 == agg_v[s], half[s], 0.0))
+        for i, part in enumerate(split3(g)):
+            gmat[i * NA : (i + 1) * NA, r * cols : (r + 1) * cols] = part
+    gx = dg(gmat[...], mo[...], NT)
+    xt[0:NA, 0:NA] = gx[0:NA] + (gx[NA : 2 * NA] + gx[2 * NA : 3 * NA])
+    xfull = xt[...]
+    inner = -(xfull + xfull.T)[0:NA]
+
     for d in range(8):
         arrive(*cond_parts(d))
         arrive(*sto_parts(d))
@@ -240,11 +263,7 @@
 
     cm, cs = extend(cond, crecv, ccorn)
     sm, ss = extend(sto, srecv, scorn)
-    last = rows - 1
     hasi = [h.astype(jnp.int32) for h in has[0:4]]
-
-    def face(a, b):
-        return 2.0 * (a * b) / (a + b)
 
     def vertical(x):
         down = jnp.where(jnp.logical_and(sub == last, hasi[1] == 0), 0.0, face(x, pltpu.roll(x, ext - 1, 0)))
@@ -298,31 +317,31 @@
                         + s_south * pltpu.roll(side, ext - 1, 0) + s_north * pltpu.roll(side, 1, 0)))
         return side + s_step * rest
 
-    in_east = jnp.where(lane < cols - 1, east, 0.0)
-    in_south = jnp.where(sub < last, south, 0.0)
-    right = pltpu.roll(agg_v, cols - 1, 1)
-    below = pltpu.roll(agg_v, last, 0)
-    half = 0.5 * diag
-    for r in range(rows):
-        s = slice(r, r + 1)
-        g = (jnp.where(sub64 == right[s], in_east[s], 0.0)
-             + jnp.where(sub64 == below[s], in_south[s], 0.0)
-             - jnp.where(sub64 == agg_v[s], half[s], 0.0))
-        for i, part in enumerate(split3(g)):
-            gmat[i * NA : (i + 1) * NA, r * cols : (r + 1) * cols] = part
-    gx = dg(gmat[...], mo[...], NT)
-    xt[0:NA, 0:NA] = gx[0:NA] + (gx[NA : 2 * NA] + gx[2 * NA : 3 * NA])
-    xfull = xt[...]
-    block = -(xfull + xfull.T)[0:NA]
-    msend[0] = block
-
+
+    for d in range(4):
+        arrive(d, agg, arecv.at[d], 16 + d)
+    agg_t = agg_v.astype(F32).T.astype(jnp.int32)
+
+    def couple(slot, own_ids, other_ids, faces, width):
+        own = jnp.where(lax.broadcasted_iota(jnp.int32, (cols, width), 0) == own_ids, 1.0, 0.0).astype(BF16)
+        other = jnp.where(lax.broadcasted_iota(jnp.int32, (NA, width), 0) == other_ids, faces, 0.0)
+        links = dot_hot(other, own, NT)
+        hi, lo = split2(-links)
+        wmat[0, slot * cols : slot * cols + NA] = hi
+        wmat[1, slot * cols : slot * cols + NA] = lo
+        return jnp.sum(links, axis=0, keepdims=True)
+
+    outer = couple(1, agg_v[last:rows], arecv[0][0:1], south[last:rows], cols)
+    outer = outer + couple(2, agg_v[0:1], arecv[1][last : rows], north[0:1], cols)
+    agg_e = arecv[2].astype(F32).T.astype(jnp.int32)
+    agg_w = arecv[3].astype(F32).T.astype(jnp.int32)
+    outer = outer + couple(3, agg_t[cols - 1 : cols], agg_e[0:1], east[0:rows].T[cols - 1 : cols], rows)
+    outer = outer + couple(4, agg_t[0:1], agg_w[cols - 1 : cols], west[0:rows].T[0:1], rows)
     def mat_copy(k):
         return copy(msend.at[k], mrecv.at[k], 44 + 4 * NX0 + k, partner[k])
 
     def vec_copy(k):
         return copy(vsend.at[k], vrecv.at[k], 44 + 4 * NX0 + LEVELS + k, partner[k])
-
-    mat_copy(0).start()
 
     lane_c = lax.broadcasted_iota(jnp.int32, (NA, cols), 1)
     lane_1 = lax.broadcasted_iota(jnp.int32, (1, cols), 1)
@@ -331,8 +350,6 @@
         d = jnp.sum(jnp.where(lane_c == sub64, mat, 0.0), axis=0, keepdims=True)
         ok = lane_1 < NA
         return jnp.where(ok, OMEGA_COARSE / jnp.where(ok, d, 1.0), 0.0)
-
-    weights = [weight(block)]
 
     def next_mat(k):
         mat_copy(k).wait_recv()
@@ -342,31 +359,25 @@
         msend[k + 1] = mat
         if k + 1 < LEVELS:
             mat_copy(k + 1).start()
-            hi, lo = split2(mat)
-            bsp[k, 0] = hi
-            bsp[k, 1] = lo
-            weights.append(weight(mat))
-
-    for d in range(4):
-        arrive(d, agg, arecv.at[d], 16 + d)
-    agg_t = agg_v.astype(F32).T.astype(jnp.int32)
-
-    def couple(slot, own_ids, other_ids, faces, width):
-        own = jnp.where(lax.broadcasted_iota(jnp.int32, (cols, width), 0) == own_ids, 1.0, 0.0).astype(BF16)
-        other = jnp.where(lax.broadcasted_iota(jnp.int32, (NA, width), 0) == other_ids, faces, 0.0)
-        hi, lo = split2(-dot_hot(other, own, NT))
-        wmat[0, slot * cols : slot * cols + NA] = hi
-        wmat[1, slot * cols : slot * cols + NA] = lo
-
+            eye = jnp.where(lane_c == sub64, 1.0, 0.0)
+            side_w = OMEGA_COARSE / jnp.sum(eye * mat, axis=1, keepdims=True)
+            one = eye - mat * weight(mat)
+            hi, lo = split2(one)
+            two = dot_parts(one[:, 0:NA], hi, lo)
+            parts = split2(dot_parts(two[:, 0:NA], hi, lo)) + split2(side_w * (eye + one + two))
+            for i in range(4):
+                bsp[k, i, 0:NA] = parts[i]
+                if i < 2:
+                    bsp[k, i, NA:cols] = jnp.zeros((cols - NA, cols), BF16)
+
+    block = inner + jnp.where(lane_c == sub64, outer, 0.0)
+    msend[0] = block
+    mat_copy(0).start()
     hi, lo = split2(block)
     wmat[0, 0:NA] = hi
     wmat[1, 0:NA] = lo
-    couple(1, agg_v[last:rows], arecv[0][0:1], south[last:rows], cols)
-    couple(2, agg_v[0:1], arecv[1][last : rows], north[0:1], cols)
-    agg_e = arecv[2].astype(F32).T.astype(jnp.int32)
-    agg_w = arecv[3].astype(F32).T.astype(jnp.int32)
-    couple(3, agg_t[cols - 1 : cols], agg_e[0:1], east[0:rows].T[cols - 1 : cols], rows)
-    couple(4, agg_t[0:1], agg_w[cols - 1 : cols], west[0:rows].T[0:1], rows)
+    weights = weight(block)
+
     for m in range(members):
         u[m, 0:rows] = guess[m]
         se[m, 0:rows] = src[m]
@@ -413,11 +424,11 @@
             mat = jnp.where(sub64 == k, pivot, mat - mat[:, k : k + 1] * pivot)
         inverse.append(jnp.where(lane_c < NA, pltpu.roll(mat, NA, 1), 0.0))
 
-    x = y0 * weights[0]
-    x = x + (y0 - level_one(0, x, lambda: next_mat(0))) * weights[0]
-    x = x + (y0 - level_one(1, x, lambda: next_mat(1))) * weights[0]
+    x = y0 * weights
+    x = x + (y0 - level_one(0, x, lambda: next_mat(0))) * weights
+    x = x + (y0 - level_one(1, x, lambda: next_mat(1))) * weights
     rem = y0 - level_one(2, x, lambda: next_mat(2))
-    sols, rhss = [x], [y0]
+    sols = [x]
     for k in range(LEVELS):
         vsend[k] = rem
         vec_copy(k).start()
@@ -425,14 +436,9 @@
             last_mat()
         vec_copy(k).wait_recv()
         y = dot_hot(rem + pltpu.roll(vrecv[k], NA, 1), qts[k], NT)
-        rhss.append(y)
         if k < LEVELS - 1:
-            apply_c = lambda z: dot_parts(z[:, 0:NA], bsp[k, 0], bsp[k, 1])
-            w = weights[k + 1]
-            x = y * w
-            for _ in range(SWEEPS - 1):
-                x = x + (y - apply_c(x)) * w
-            rem = y - apply_c(x)
+            rem = dot_parts(y, bsp[k, 0], bsp[k, 1], NT)
+            x = dot_parts(y[:, 0:NA], bsp[k, 2, 0:NA], bsp[k, 3, 0:NA])
         else:
             x = lax.dot_general(y[:, 0:NA], inverse[0], NN, precision=lax.Precision.HIGHEST,
                                 preferred_element_type=F32)
@@ -440,12 +446,11 @@
     lane_m = lax.broadcasted_iota(jnp.int32, (members, cols), 1)
     for k in reversed(range(LEVELS)):
         x = sols[k] + jnp.where(lane_m < NA, dot_hot(x, qts[k], NN), 0.0)
-        for i in range(SWEEPS):
-            if k > 0:
-                applied = dot_parts(x[:, 0:NA], bsp[k - 1, 0], bsp[k - 1, 1])
-            else:
-                applied = level_one(SWEEPS + i, x)
-            x = x + (rhss[k] - applied) * weights[k]
+        if k > 0:
+            x = sols[k] + dot_parts(x[:, 0:NA], bsp[k - 1, 0, 0:NA], bsp[k - 1, 1, 0:NA])
+        else:
+            for i in range(SWEEPS):
+                x = x + (y0 - level_one(SWEEPS + i, x)) * weights
 
     for r in range(rows):
         part = dot_hot(x[:, 0:NA], mo[:, r * cols : (r + 1) * cols], NN)
@@ -508,7 +513,7 @@
             pltpu.VMEM((LEVELS + 1, members, cols), F32),
             pltpu.VMEM((LEVELS, members, cols), F32),
             pltpu.VMEM((2, 5 * cols, cols), BF16),
-            pltpu.VMEM((LEVELS - 1, 2, NA, cols), BF16),
+            pltpu.VMEM((LEVELS - 1, 4, cols, cols), BF16),
             pltpu.VMEM((LEVELS, cols, cols), BF16),
             pltpu.SemaphoreType.DMA((slots,)),
             pltpu.SemaphoreType.DMA((slots,)),

time: 65.4 us -> 62.9 us (0.962)
  Pallas kernels: 62.1 us -> 59.7 us
    pallas_call x1, Pallas kernels: 62.1 us -> 59.7 us  [shards(): pl.pallas_call(functools.partial(kernel, n_row, n_col), out_shape=(jax.Sh...]
where the time goes in v3:
time: 62.9 us; the launch traced here: 62.8 us
  Pallas kernels  59.7 us (95%)
  local copies, waits for them, and re-layouts  2.42 us (4%)
  between operations  0.65 us (1%)
    pallas_call x1, Pallas kernels, shards(): pl.pallas_call(functools.partial(kernel, n_row, n_col), out_shape=(jax.Sh...  59.7 us
    unnamed x4, local copies, waits for them, and re-layouts  2.42 us

profile of v3, /device:TPU:0, one launch (start us, length us, event | category | flops | bytes accessed | tf_op | source)
XLA Modules:
  0.0 62.8 jit_solution(15125762066468860517)
XLA Ops:
  0.6 59.7 %shard_map.77 = (f32[16,32,128]{2,1,0:T(8,128)}, f32[16,32,128]{2,1,0:T(8,128)}) custom-call(f32[16,32,128]{2,1,0:T(8,128)} %src.1, f32[16,32,128]{2,1,0:T(8,128)} %guess.1, f32[32,128]{1,0:T(8,128)} %cond.1, f32[32,128]{1,0:T(8,128)} %sto.1, s32[32,128]{1,0:T(8,128)} %agg.1, s32[4,128]{1,0:T(4,128)} %bitcast.1), custom_call_target="tpu_custom_call" | custom-call | tf_op jit(solution)/shard_map/pallas_call | solution.py:486
  60.3 0.0 copy-start
  60.3 1.7 %copy.10 = f32[16,32,128]{2,1,0:T(8,128)} copy(f32[16,32,128]{2,1,0:T(8,128)} %get-tuple-element.4) | data formatting | bytes 524288
  62.1 0.0 copy-done
  62.1 0.7 %copy.11 = f32[16,32,128]{2,1,0:T(8,128)} copy(f32[16,32,128]{2,1,0:T(8,128)S(1)} %copy-done) | data formatting | bytes 524288
Async XLA Ops:
  60.3 1.7 %copy-start = (f32[16,32,128]{2,1,0:T(8,128)S(1)}, f32[16,32,128]{2,1,0:T(8,128)}, u32[]{:S(2)}) copy-start(f32[16,32,128]{2,1,0:T(8,128)} %get-tuple-element.5) | copy-start | bytes 786436

commit v4 on v3

--- a/solution.py
+++ b/solution.py
@@ -392,6 +392,7 @@
         left[m] = rest
 
     apply_field(side, rows, keep_left)
+    next_mat(0)
     for r in range(rows):
         for i, part in enumerate(split3(left[:, r, :])):
             rlhs[i * members : (i + 1) * members, r * cols : (r + 1) * cols] = part
@@ -425,15 +426,13 @@
         inverse.append(jnp.where(lane_c < NA, pltpu.roll(mat, NA, 1), 0.0))
 
     x = y0 * weights
-    x = x + (y0 - level_one(0, x, lambda: next_mat(0))) * weights
-    x = x + (y0 - level_one(1, x, lambda: next_mat(1))) * weights
-    rem = y0 - level_one(2, x, lambda: next_mat(2))
+    x = x + (y0 - level_one(0, x, lambda: next_mat(1))) * weights
+    x = x + (y0 - level_one(1, x, lambda: next_mat(2))) * weights
+    rem = y0 - level_one(2, x, last_mat)
     sols = [x]
     for k in range(LEVELS):
         vsend[k] = rem
         vec_copy(k).start()
-        if k == 1:
-            last_mat()
         vec_copy(k).wait_recv()
         y = dot_hot(rem + pltpu.roll(vrecv[k], NA, 1), qts[k], NT)
         if k < LEVELS - 1:

time: 62.9 us -> 61.4 us (0.976)
  Pallas kernels: 59.7 us -> 58 us
    pallas_call x1, Pallas kernels: 59.7 us -> 58 us  [shards(): pl.pallas_call(functools.partial(kernel, n_row, n_col), out_shape=(jax.Sh...]
where the time goes in v4:
time: 61.4 us; the launch traced here: 61.1 us
  Pallas kernels  58 us (94%)
  local copies, waits for them, and re-layouts  2.42 us (4%)
  between operations  0.65 us (1%)
    pallas_call x1, Pallas kernels, shards(): pl.pallas_call(functools.partial(kernel, n_row, n_col), out_shape=(jax.Sh...  58 us
    unnamed x4, local copies, waits for them, and re-layouts  2.42 us

profile of v4, /device:TPU:0, one launch (start us, length us, event | category | flops | bytes accessed | tf_op | source)
XLA Modules:
  0.0 61.1 jit_solution(8912127137560175837)
XLA Ops:
  0.6 58.0 %shard_map.77 = (f32[16,32,128]{2,1,0:T(8,128)}, f32[16,32,128]{2,1,0:T(8,128)}) custom-call(f32[16,32,128]{2,1,0:T(8,128)} %src.1, f32[16,32,128]{2,1,0:T(8,128)} %guess.1, f32[32,128]{1,0:T(8,128)} %cond.1, f32[32,128]{1,0:T(8,128)} %sto.1, s32[32,128]{1,0:T(8,128)} %agg.1, s32[4,128]{1,0:T(4,128)} %bitcast.1), custom_call_target="tpu_custom_call" | custom-call | tf_op jit(solution)/shard_map/pallas_call | solution.py:485
  58.6 0.0 copy-start
  58.6 1.7 %copy.10 = f32[16,32,128]{2,1,0:T(8,128)} copy(f32[16,32,128]{2,1,0:T(8,128)} %get-tuple-element.4) | data formatting | bytes 524288
  60.3 0.0 copy-done
  60.4 0.7 %copy.11 = f32[16,32,128]{2,1,0:T(8,128)} copy(f32[16,32,128]{2,1,0:T(8,128)S(1)} %copy-done) | data formatting | bytes 524288
Async XLA Ops:
  58.6 1.7 %copy-start = (f32[16,32,128]{2,1,0:T(8,128)S(1)}, f32[16,32,128]{2,1,0:T(8,128)}, u32[]{:S(2)}) copy-start(f32[16,32,128]{2,1,0:T(8,128)} %get-tuple-element.5) | copy-start | bytes 786436
